TPU v7x, 32 devices: a whole 2x2x4 slice. The times are simulated.
32 devices in a mesh: groups: 2 (over y), inner: 4 (over z), outer: 4 (over x, core).
Axes of the slice: x: 2, y: 2, z: 4, core: 2. Of those that a mesh axis runs over, the one named last changes fastest.
Arguments:
- queries: bfloat16 [8192, 1024], P(('groups', 'outer', 'inner')), parts along dimension 0, may hold values from -6 to 6
- keys: bfloat16 [8192, 1024], P(('groups', 'outer', 'inner')), parts along dimension 0, may hold values from -6 to 6
- values: bfloat16 [8192, 1024], P(('groups', 'outer', 'inner')), parts along dimension 0, may hold values from -6 to 6
- retain: float32 [8192, 8], P(('groups', 'outer', 'inner')), parts along dimension 0, may hold values from 0.4 to 1
- step: float32 [8192, 8], P(('groups', 'outer', 'inner')), parts along dimension 0, may hold values from 0.000625 to 0.0125
- momentum: float32 [8192, 8], P(('groups', 'outer', 'inner')), parts along dimension 0, may hold values from 0.97 to 0.99
- init_memory: float32 [8, 128, 128], replicated, may hold values from -0.1875 to 0.1875
- init_momentum: float32 [8, 128, 128], replicated, may hold values from -0.1875 to 0.1875
Outputs:
- retrieved: bfloat16 [8192, 1024], P(('groups', 'outer', 'inner')), parts along dimension 0
There are 2 independent parts, one for each index of `groups`. A program takes and returns all parts, laid end to end along the dimension named above; an argument that names none is the same for every part. Nothing has to cross between parts.
All inputs are finite; a program needn't handle non-finite values.
Results may differ from a plain program's by a relative error of at most 0.001.
Values sent between devices are 32-bit elements; how exact they have to be, the bound alone decides.
No kernel may reach another device: no remote copies, remote signals or barrier semaphores. Data moves between devices by JAX's collectives and lax.ppermute only.
A program may use at most 256 MiB of HBM per device.

v0:
```python
import jax
import jax.numpy as jnp
from jax import lax
from jax.sharding import PartitionSpec as P


def carried_in(value, axis, join, neutral):
    count, mine = (lax.axis_size(axis), lax.axis_index(axis))
    pieces = jax.tree.map(lambda part: lax.all_gather(part, axis), value)
    total = jax.tree.map(
        lambda part, zero: jnp.full_like(part, 0) + jnp.asarray(zero, part.dtype), value, neutral
    )

    def turn(position, total):
        longer = join(total, jax.tree.map(lambda part: part[position], pieces))
        return jax.tree.map(lambda new, old: jnp.where(position < mine, new, old), longer, total)

    return lax.fori_loop(0, count - 1, turn, total)


def from_root(block, axis, owner):
    block = jnp.where(lax.axis_index(axis) == owner, block, jnp.zeros_like(block))
    return lax.psum(block, axis)


def unit_rows(source, heads):
    rows = source.astype(jnp.float32).reshape(source.shape[0], heads, -1)
    return rows * lax.rsqrt(jnp.sum(rows * rows, -1, keepdims=True) + 1e-06)


def block_terms(queries, keys, values, retain, step, momentum):
    length = queries.shape[0]
    heads = retain.shape[1]
    precise = lax.Precision.HIGHEST
    query_unit = unit_rows(queries, heads)
    key_unit = unit_rows(keys, heads)
    value_rows = values.astype(jnp.float32).reshape(length, heads, -1)
    key_width = key_unit.shape[2]
    log_retain = jnp.cumsum(jnp.log(retain), 0).T
    log_moment = jnp.cumsum(jnp.log(momentum), 0).T
    position = jnp.arange(length)
    causal = (position[:, None] >= position[None, :])[None]
    retain_decay = jnp.where(
        causal,
        jnp.exp(jnp.where(causal, log_retain[:, :, None] - log_retain[:, None, :], 0.0)),
        0.0,
    )
    momentum_decay = jnp.where(
        causal,
        jnp.exp(jnp.where(causal, log_moment[:, :, None] - log_moment[:, None, :], 0.0)),
        0.0,
    )
    weights = jnp.einsum("htu,hur->htr", retain_decay, momentum_decay, precision=precise)
    carry_scale = jnp.einsum("htu,hu->ht", retain_decay, jnp.exp(log_moment), precision=precise)
    scores = jnp.einsum("thd,rhd->htr", query_unit, key_unit, precision=precise)
    step_rows = step.T
    mixing = scores * weights * step_rows[:, None, :]
    memory_weight = weights[:, -1, :] * step_rows
    moment_weight = jnp.exp(log_moment[:, -1:] - log_moment) * step_rows
    memory_gram = jnp.einsum(
        "rhd,hr,rhe->hde", key_unit, memory_weight, key_unit, precision=precise
    )
    moment_gram = jnp.einsum(
        "rhd,hr,rhe->hde", key_unit, moment_weight, key_unit, precision=precise
    )
    identity = jnp.eye(key_width, dtype=jnp.float32)[None]
    retain_end = jnp.exp(log_retain[:, -1])[:, None, None]
    moment_end = jnp.exp(log_moment[:, -1])[:, None, None]
    carry_end = carry_scale[:, -1][:, None, None]
    upper_rows = jnp.concatenate([retain_end * identity - memory_gram, -moment_gram], axis=2)
    lower_rows = jnp.concatenate([carry_end * identity, moment_end * identity], axis=2)
    transition = jnp.concatenate([upper_rows, lower_rows], axis=1)
    memory_write = jnp.einsum(
        "rhd,hr,rhe->hde", value_rows, memory_weight, key_unit, precision=precise
    )
    moment_write = jnp.einsum(
        "rhd,hr,rhe->hde", value_rows, moment_weight, key_unit, precision=precise
    )
    offset = jnp.concatenate([memory_write, moment_write], axis=2)
    local_terms = (query_unit, key_unit, value_rows, jnp.exp(log_retain), carry_scale, mixing)
    return (transition, offset, local_terms)


def block_output(carried, local_terms):
    query_unit, key_unit, value_rows, retain_scale, carry_scale, mixing = local_terms
    precise = lax.Precision.HIGHEST
    key_width = query_unit.shape[2]
    memory = carried[:, :, :key_width]
    moment_part = carried[:, :, key_width:]
    residual = jnp.einsum("rhd,hed->hre", key_unit, memory, precision=precise) - jnp.transpose(
        value_rows, (1, 0, 2)
    )
    result = retain_scale[:, :, None] * jnp.einsum(
        "thd,hed->hte", query_unit, memory, precision=precise
    )
    result = result + carry_scale[:, :, None] * jnp.einsum(
        "thd,hed->hte", query_unit, moment_part, precision=precise
    )
    result = result - jnp.einsum("htr,hre->hte", mixing, residual, precision=precise)
    return jnp.transpose(result, (1, 0, 2)).reshape(query_unit.shape[0], -1).astype(jnp.bfloat16)


def advance_state(carried, transition, offset):
    return jnp.einsum("hij,hjk->hik", carried, transition, precision=lax.Precision.HIGHEST) + offset


def compose(earlier, later):
    joined = jnp.einsum("hij,hjk->hik", earlier[0], later[0], precision=lax.Precision.HIGHEST)
    return (joined, advance_state(earlier[1], later[0], later[1]))


def apply_earlier(gathered, first_state):
    my_group = lax.axis_index("outer")

    def advance_group(index, carried):
        moved = advance_state(carried, gathered[0][index], gathered[1][index])
        return jnp.where(index < my_group, moved, carried)

    return lax.fori_loop(0, gathered[0].shape[0], advance_group, first_state)


def local(queries, keys, values, retain, step, momentum, init_memory, init_momentum):
    transition, offset, local_terms = block_terms(queries, keys, values, retain, step, momentum)
    identity_maps = (
        jnp.broadcast_to(jnp.eye(transition.shape[1], dtype=jnp.float32), transition.shape),
        jnp.zeros_like(offset),
    )
    before = carried_in((transition, offset), "inner", compose, identity_maps)
    through = compose(before, (transition, offset))
    first_state = jnp.concatenate([init_memory, init_momentum], axis=2)
    last_inner = lax.axis_size("inner") - 1
    group_map = (
        from_root(through[0], "inner", last_inner),
        from_root(through[1], "inner", last_inner),
    )
    gathered = (
        lax.all_gather(group_map[0][None], "outer", axis=0, tiled=True),
        lax.all_gather(group_map[1][None], "outer", axis=0, tiled=True),
    )
    entry_state = apply_earlier(gathered, first_state)
    block_state = advance_state(entry_state, before[0], before[1])
    return block_output(block_state, local_terms)


def solution(mesh):
    placed = (
        P(("groups", "outer", "inner"), None),
        P(("groups", "outer", "inner"), None),
        P(("groups", "outer", "inner"), None),
        P(("groups", "outer", "inner"), None),
        P(("groups", "outer", "inner"), None),
        P(("groups", "outer", "inner"), None),
        P(),
        P(),
    )
    return jax.shard_map(
        local,
        mesh=mesh,
        in_specs=placed,
        out_specs=P(("groups", "outer", "inner"), None),
        check_vma=False,
    )
```

profile of v0, /device:TPU:1, one launch (start us, length us, event | category | flops | bytes accessed | tf_op | source)
XLA Modules:
  0.0 601.1 jit_solution(4477719836671399538)
XLA Ops:
  10.5 2.9 fusion.39
  29.2 2.6 copy.125
  41.2 73.6 %all-gather.13.cloned.1.call-done = f32[32,128,256]{2,1,0:T(8,128)} async-done(((f32[8,128,256]{2,1,0:T(8,128)}), f32[32,128,256]{2,1,0:T(8,128)}) %all-gather.13.cloned.1.call-update) | async-done | bytes 4194320 | tf_op jit(solution)/shard_map/all_gather | solution.py:9
  114.8 150.0 %all-gather.11.cloned.1.call-done = f32[32,256,256]{2,1,0:T(8,128)} async-done(((f32[8,256,256]{2,1,0:T(8,128)}), f32[32,256,256]{2,1,0:T(8,128)}) %all-gather.11.cloned.1.call-update) | async-done | bytes 8388624 | tf_op jit(solution)/shard_map/all_gather | solution.py:9
  265.0 49.7 %while.30 = (s32[]{:T(128)}, f32[8,256,256]{1,2,0:T(8,128)S(1)}, f32[8,128,256]{1,2,0:T(8,128)}, s32[]{:T(128)}, f32[4,8,256,256]{3,2,1,0:T(8,128)}, /*index=5*/f32[4,8,128,256]{3,2,1,0:T(8,128)}, s32[]{:T(128)}, s32[]{:T(128)}) while((s32[]{:T(128)}, f32[8,256,256]{1,2,0:T(8,128)S(1)}, f32[8,128,256]{1,2,0:T(8,128)}, s32[]{:T(128)}, ...), condition=%wide.region_7.8_spmd.clone, body=%wide.region_6.7_spmd.clone.sunk | while | flops 2417491968 | bytes 25168492 | solution.py:18
  270.1 6.1 %fusion.112 = f32[8,128,256]{1,2,0:T(8,128)} fusion(f32[4,8,256,256]{3,2,1,0:T(8,128)} %get-tuple-element.387, s32[]{:T(128)} %get-tuple-element.375, f32[1,8,128,256]{2,3,1,0:T(8,128)S(1)} %copy.193, f32[8,128,256]{1,2,0:T(8,128)S(1)} %copy.218, pred[]{:T(512)S(6)} %compare.3, pred[]{:T(512)S(6)} %lt.44), kind=kOutput, calls=%fused_computation.17.clone.1 | convolution fusion | flops 806354944 | bytes 6293504 | tf_op jit(solution)/shard_map/while/body/eval_jaxpr/hij,hjk->hik/dot_general | solution.py:104
  276.4 5.1 bitcast_select_fusion.2
  286.6 6.1 %fusion.112 = f32[8,128,256]{1,2,0:T(8,128)} fusion(f32[4,8,256,256]{3,2,1,0:T(8,128)} %get-tuple-element.387, s32[]{:T(128)} %get-tuple-element.375, f32[1,8,128,256]{2,3,1,0:T(8,128)S(1)} %copy.193, f32[8,128,256]{1,2,0:T(8,128)S(1)} %copy.218, pred[]{:T(512)S(6)} %compare.3, pred[]{:T(512)S(6)} %lt.44), kind=kOutput, calls=%fused_computation.17.clone.1 | convolution fusion | flops 806354944 | bytes 6293504 | tf_op jit(solution)/shard_map/while/body/eval_jaxpr/hij,hjk->hik/dot_general | solution.py:104
  292.9 5.1 bitcast_select_fusion.2
  303.1 6.1 %fusion.112 = f32[8,128,256]{1,2,0:T(8,128)} fusion(f32[4,8,256,256]{3,2,1,0:T(8,128)} %get-tuple-element.387, s32[]{:T(128)} %get-tuple-element.375, f32[1,8,128,256]{2,3,1,0:T(8,128)S(1)} %copy.193, f32[8,128,256]{1,2,0:T(8,128)S(1)} %copy.218, pred[]{:T(512)S(6)} %compare.3, pred[]{:T(512)S(6)} %lt.44), kind=kOutput, calls=%fused_computation.17.clone.1 | convolution fusion | flops 806354944 | bytes 6293504 | tf_op jit(solution)/shard_map/while/body/eval_jaxpr/hij,hjk->hik/dot_general | solution.py:104
  309.4 5.1 bitcast_select_fusion.2
  314.8 5.2 fusion.49
  320.0 4.8 select_bitcast_fusion
  324.9 119.5 %all-reduce.3.cloned.1.call-done = (f32[1,8,256,256]{3,2,1,0:T(8,128)}, f32[1,8,128,256]{2,3,1,0:T(8,128)}) async-done(((f32[1,8,256,256]{3,2,1,0:T(8,128)}, f32[1,8,128,256]{2,3,1,0:T(8,128)}), (f32[1,8,256,256]{3,2,1,0:T(8,128)}, f32[1,8,128,256]{2,3,1,0:T(8,128)})) %all-reduce.3.cloned.1.call-update) | async-done | bytes 3145744 | tf_op jit(solution)/shard_map/psum | solution.py:23
  444.4 2.5 copy.133
  451.4 5.1 fusion.66
  457.9 23.1 %all-gather.9.cloned.1.call-done = f32[4,8,128,256]{3,2,1,0:T(8,128)} async-done(((f32[1,8,128,256]{3,2,1,0:T(8,128)}), f32[4,8,128,256]{3,2,1,0:T(8,128)}) %all-gather.9.cloned.1.call-update) | async-done | bytes 4194320 | tf_op jit(solution)/shard_map/all_gather | solution.py:138
  481.0 59.7 %all-gather.7.cloned.1.call-done = f32[4,8,256,256]{3,2,1,0:T(8,128)} async-done(((f32[1,8,256,256]{3,2,1,0:T(8,128)}), f32[4,8,256,256]{3,2,1,0:T(8,128)}) %all-gather.7.cloned.1.call-update) | async-done | bytes 8388624 | tf_op jit(solution)/shard_map/all_gather | solution.py:137
  540.8 41.4 %while.29 = (s32[]{:T(128)}, f32[8,128,256]{1,2,0:T(8,128)}, s32[]{:T(128)}, f32[4,8,256,256]{3,2,1,0:T(8,128)}, f32[4,8,128,256]{3,2,1,0:T(8,128)}, /*index=5*/s32[]{:T(128)}) while((s32[]{:T(128)}, f32[8,128,256]{1,2,0:T(8,128)}, s32[]{:T(128)}, f32[4,8,256,256]{3,2,1,0:T(8,128)}, f32[4,8,128,256]{3,2,1,0:T(8,128)}, ...), condition=%wide.region_11.12_spmd, body=%wide.region_10.11_spmd.sunk | while | flops 805830656 | bytes 16777840 | solution.py:119
  545.2 6.1 %fusion.107 = f32[8,128,256]{1,2,0:T(8,128)} fusion(f32[8,128,256]{1,2,0:T(8,128)S(1)} %copy.216, f32[4,8,256,256]{3,2,1,0:T(8,128)} %get-tuple-element.406, s32[]{:T(128)} %get-tuple-element.397, f32[1,8,128,256]{2,3,1,0:T(8,128)S(1)} %copy-done, pred[]{:T(512)S(6)} %lt.43), kind=kOutput, calls=%fused_computation.5.clone.1 | convolution fusion | flops 805830656 | bytes 6291969 | tf_op jit(solution)/shard_map/while/body/eval_jaxpr/hij,hjk->hik/dot_general | solution.py:104
  555.5 6.1 %fusion.107 = f32[8,128,256]{1,2,0:T(8,128)} fusion(f32[8,128,256]{1,2,0:T(8,128)S(1)} %copy.216, f32[4,8,256,256]{3,2,1,0:T(8,128)} %get-tuple-element.406, s32[]{:T(128)} %get-tuple-element.397, f32[1,8,128,256]{2,3,1,0:T(8,128)S(1)} %copy-done, pred[]{:T(512)S(6)} %lt.43), kind=kOutput, calls=%fused_computation.5.clone.1 | convolution fusion | flops 805830656 | bytes 6291969 | tf_op jit(solution)/shard_map/while/body/eval_jaxpr/hij,hjk->hik/dot_general | solution.py:104
  565.8 6.1 %fusion.107 = f32[8,128,256]{1,2,0:T(8,128)} fusion(f32[8,128,256]{1,2,0:T(8,128)S(1)} %copy.216, f32[4,8,256,256]{3,2,1,0:T(8,128)} %get-tuple-element.406, s32[]{:T(128)} %get-tuple-element.397, f32[1,8,128,256]{2,3,1,0:T(8,128)S(1)} %copy-done, pred[]{:T(512)S(6)} %lt.43), kind=kOutput, calls=%fused_computation.5.clone.1 | convolution fusion | flops 805830656 | bytes 6291969 | tf_op jit(solution)/shard_map/while/body/eval_jaxpr/hij,hjk->hik/dot_general | solution.py:104
  576.1 6.1 %fusion.107 = f32[8,128,256]{1,2,0:T(8,128)} fusion(f32[8,128,256]{1,2,0:T(8,128)S(1)} %copy.216, f32[4,8,256,256]{3,2,1,0:T(8,128)} %get-tuple-element.406, s32[]{:T(128)} %get-tuple-element.397, f32[1,8,128,256]{2,3,1,0:T(8,128)S(1)} %copy-done, pred[]{:T(512)S(6)} %lt.43), kind=kOutput, calls=%fused_computation.5.clone.1 | convolution fusion | flops 805830656 | bytes 6291969 | tf_op jit(solution)/shard_map/while/body/eval_jaxpr/hij,hjk->hik/dot_general | solution.py:104
  582.2 4.0 convolution_add_fusion
  (165 shorter events, 75.1 us)
Async XLA Ops:
  6.5 108.3 %all-gather.13.cloned.1.call-start = ((), (), s32[]{:S(2)}) async-start(), calls=%async_computation.3 | async-start | bytes 5242880 | tf_op jit(solution)/shard_map/all_gather | solution.py:9
  6.6 6.9 %copy-start.25 = (pred[256,256]{1,0:T(8,128)(4,1)}, pred[256,256]{1,0:T(8,128)(4,1)S(1)}, u32[]{:S(2)}) copy-start(pred[256,256]{1,0:T(8,128)(4,1)S(1)} %iota_compare_fusion) | copy-start | bytes 196612
  8.2 5.3 copy-start.28
  10.5 3.0 copy-start.31
  10.5 3.0 copy-start.27
  10.5 4.4 copy-start.21
  20.4 16.3 %copy-start.2 = (f32[256,8,128]{2,1,0:T(8,128)}, f32[256,8,128]{2,1,0:T(8,128)S(1)}, u32[]{:S(2)}) copy-start(f32[256,8,128]{2,1,0:T(8,128)S(1)} %get-tuple-element.291) | copy-start | bytes 3145732
  29.2 3.2 copy-start.32
  29.2 3.2 copy-start.26
  29.2 3.2 copy-start.29
  29.2 3.2 copy-start.30
  31.8 233.0 %all-gather.11.cloned.1.call-start = ((), (), s32[]{:S(2)}) async-start(), calls=%async_computation.2 | async-start | bytes 10485760 | tf_op jit(solution)/shard_map/all_gather | solution.py:9
  35.3 2.9 copy-start.8
  35.3 2.9 copy-start.10
  41.0 403.4 %all-reduce.3.cloned.1.call-start = ((), (), s32[]{:S(2)}) async-start(), calls=%async_computation.4 | async-start | bytes 6291456 | tf_op jit(solution)/shard_map/psum | solution.py:23
  314.7 5.2 copy-start.9
  314.7 5.2 copy-start.11
  314.7 5.2 copy-start.13
  314.8 5.2 copy-start.15
  324.8 156.2 %all-gather.9.cloned.1.call-start = ((), (), s32[]{:S(2)}) async-start(), calls=%async_computation.1 | async-start | bytes 5242880 | tf_op jit(solution)/shard_map/all_gather | solution.py:138
  446.9 93.8 %all-gather.7.cloned.1.call-start = ((), (), s32[]{:S(2)}) async-start(), calls=%async_computation | async-start | bytes 10485760 | tf_op jit(solution)/shard_map/all_gather | solution.py:137
  451.4 5.1 copy-start.1
  582.2 4.0 copy-start.4
  586.2 2.5 copy-start.17
  (17 other events, 23.7 us)
Sparse Core Ops, SparseCore 0:
  31.9 82.8 all-gather.12
  116.4 148.3 all-gather.10
  324.9 119.3 all-reduce.2
  447.0 33.9 all-gather.8
  482.4 58.2 all-gather.6
where the time goes:
time: 609 us; the launch traced here: 601 us
  waiting for transfers between devices  426 us (70%)
  matrix products  93.8 us (15%)
  local copies, waits for them, and re-layouts  56.5 us (9%)
  between operations  14.2 us (2%)
  other arithmetic  8.6 us (1%)
    all_gather x2, waiting for transfers between devices, carried_in(): pieces = jax.tree.map(lambda part: lax.all_gather(part, axis), value)  224 us
    psum x1, waiting for transfers between devices, from_root(): return lax.psum(block, axis)  120 us
    all_gather x1, waiting for transfers between devices, local(): lax.all_gather(group_map[0][None], 'outer', axis=0, tiled=True)  59.7 us
    dot_general x9, matrix products, advance_state(): jnp.einsum('hij,hjk->hik', carried, transition, precision=lax.Precision.H...  51.8 us
    all_gather x1, waiting for transfers between devices, local(): lax.all_gather(group_map[1][None], 'outer', axis=0, tiled=True)  23.1 us
    dot_general x4, matrix products, compose(): jnp.einsum('hij,hjk->hik', earlier[0], later[0], precision=lax.Precision....  20.2 us
  transfers between devices with their start and end apart: 5, of which 5 were waited for; matrix products, arithmetic and copies ran while one was open for 3% of the time, Pallas kernels for 0%

commit v1 on v0

v1 whole, which is shorter than its diff:
```python
import functools

import jax
import jax.numpy as jnp
from jax import lax
from jax.experimental import pallas as pl
from jax.experimental.pallas import tpu as pltpu
from jax.sharding import PartitionSpec as P

TAIL = 8
EPS = 1e-06
EXACT = lax.Precision.HIGHEST


def halves(x):
    high = x.astype(jnp.bfloat16)
    return high, (x - high.astype(jnp.float32)).astype(jnp.bfloat16)


def mul(a, b, dims):
    return lax.dot_general(a, b, (dims, ((), ())), preferred_element_type=jnp.float32)


def mul_tn(a, b):
    return mul(a, b, ((0,), (0,)))


def mul_nt(a, b):
    return mul(a, b, ((1,), (1,)))


def mul_nn(a, b):
    return mul(a, b, ((1,), (0,)))


def grid_ids(shape):
    return lax.broadcasted_iota(jnp.int32, shape, 0), lax.broadcasted_iota(jnp.int32, shape, 1)


def running_logs(retain, momentum):
    length = retain.shape[0]
    row, col = grid_ids((length, length))
    lower = (row >= col).astype(jnp.float32)
    log_retain = jnp.dot(lower, jnp.log(retain), precision=EXACT, preferred_element_type=jnp.float32)
    log_moment = jnp.dot(lower, jnp.log(momentum), precision=EXACT, preferred_element_type=jnp.float32)
    return log_retain, log_moment


def map_kernel(heads, width, k_ref, v_ref, retain_ref, step_ref, momentum_ref, out_ref):
    length = k_ref.shape[0]
    step = step_ref[...]
    log_retain, log_moment = running_logs(retain_ref[...], momentum_ref[...])
    row, col = grid_ids((length, length))
    upper = (row <= col).astype(jnp.float32)
    decay = jnp.exp(log_moment)
    reach = jnp.exp(log_retain[length - 1 :, :] - log_retain) * decay
    suffix = jnp.dot(upper, reach, precision=EXACT, preferred_element_type=jnp.float32)
    memory_weight = suffix / decay * step
    moment_weight = jnp.exp(log_moment[length - 1 :, :] - log_moment) * step
    retain_end = jnp.exp(log_retain[length - 1 :, :])
    moment_end = decay[length - 1 :, :]
    carry_end = suffix[:1, :]
    drow, dcol = grid_ids((width, width))
    keep = drow <= dcol
    diagonal = drow == dcol
    for h in range(heads):
        lanes = slice(h * width, (h + 1) * width)
        keys = k_ref[:, lanes]
        values = v_ref[:, lanes]
        wide = keys.astype(jnp.float32)
        scale = lax.rsqrt(jnp.sum(wide * wide, -1, keepdims=True) + EPS)
        weight_m = memory_weight[:, h : h + 1] * scale
        weight_s = moment_weight[:, h : h + 1] * scale
        write = jnp.concatenate([wide * weight_m, wide * weight_s], axis=1)
        high, low = halves(write)
        offset = mul_tn(values, high) + mul_tn(values, low)
        high, low = halves(write * scale)
        gram = mul_tn(keys, high) + mul_tn(keys, low)
        moment_gram = gram[:, width:]
        out_ref[h, :width, :] = jnp.where(keep, gram[:, :width], moment_gram)
        out_ref[h, width : 2 * width, :] = offset[:, :width]
        out_ref[h, 2 * width : 3 * width, :] = offset[:, width:]
        on_diagonal = jnp.sum(jnp.where(diagonal, moment_gram, 0.0), axis=0, keepdims=True)
        wide_row = lambda x: jnp.broadcast_to(x[:, h : h + 1], (1, width))
        out_ref[h, 3 * width :, :] = jnp.concatenate(
            [
                on_diagonal,
                wide_row(retain_end),
                wide_row(moment_end),
                wide_row(carry_end),
                jnp.zeros((TAIL - 4, width), jnp.float32),
            ],
            axis=0,
        )


def read_kernel(
    heads, width, q_ref, k_ref, v_ref, retain_ref, step_ref, momentum_ref, high_ref, low_ref, base_ref
):
    length = k_ref.shape[0]
    log_retain, log_moment = running_logs(retain_ref[...], momentum_ref[...])
    row, col = grid_ids((length, length))
    causal = row >= col
    lower = causal.astype(jnp.bfloat16)
    identity = (row == col).astype(jnp.float32)
    flip = lambda x: lax.dot_general(
        x, identity, (((0,), (0,)), ((), ())), precision=EXACT, preferred_element_type=jnp.float32
    )
    log_gap = flip(log_moment - log_retain)
    step_rows = flip(step_ref[...] * jnp.exp(-log_moment))
    retain_scale = jnp.exp(log_retain)
    ones = jnp.ones((8, width), jnp.bfloat16)
    for h in range(heads):
        lanes = slice(h * width, (h + 1) * width)
        queries, keys, values = q_ref[:, lanes], k_ref[:, lanes], v_ref[:, lanes]
        wide_q = queries.astype(jnp.float32)
        wide_k = keys.astype(jnp.float32)
        query_scale = lax.rsqrt(jnp.sum(wide_q * wide_q, -1, keepdims=True) + EPS)
        high, low = halves(wide_k * wide_k)
        key_scale = lax.rsqrt((mul_nt(ones, high) + mul_nt(ones, low))[:1, :] + EPS)
        gap = log_retain[:, h : h + 1] + log_gap[h : h + 1, :]
        reach = jnp.exp(jnp.where(causal, gap, -1e30))
        high, low = halves(reach)
        weights = mul_nn(high, lower) + mul_nn(low, lower)
        mixing = mul_nt(queries, keys) * weights * (step_rows[h : h + 1, :] * key_scale)
        high, low = halves(mixing)
        base_ref[h] = query_scale * (mul_nn(high, values) + mul_nn(low, values))
        high, low = halves(mixing * key_scale)
        seen = mul_nn(high, keys) + mul_nn(low, keys)
        unit_q = query_scale * wide_q
        reads = jnp.concatenate(
            [retain_scale[:, h : h + 1] * unit_q - query_scale * seen, weights[:, :1] * unit_q], axis=1
        )
        high, low = halves(reads)
        high_ref[h] = high
        low_ref[h] = low


def scan_kernel(width, keep_states, merged, flag_ref, maps_ref, entry_ref, *refs):
    if merged:
        other_ref, *refs = refs
        entry = jnp.where(flag_ref[0] > 0, other_ref[...], entry_ref[...])
    else:
        entry = entry_ref[...]
    blocks = maps_ref.shape[0]
    row, col = grid_ids((width, width))
    if not keep_states and merged:
        refs[1][...] = entry
    state = entry
    for b in range(blocks):
        if keep_states:
            refs[0][b] = state
            if b == blocks - 1:
                return
        packed = maps_ref[b, :width, :]
        flipped = packed.T
        tail = maps_ref[b, 3 * width :, :]
        gram = jnp.concatenate(
            [
                jnp.where(row <= col, packed, flipped),
                jnp.where(row == col, tail[:1, :], jnp.where(row > col, packed, flipped)),
            ],
            axis=1,
        )
        gram_high, gram_low = halves(gram)
        memory, moment = state[:, :width], state[:, width:]
        high, low = halves(memory)
        seen = mul_nn(high, gram_high) + (mul_nn(high, gram_low) + mul_nn(low, gram_high))
        new_memory = (
            tail[1:2, :] * memory + tail[3:4, :] * moment + maps_ref[b, width : 2 * width, :] - seen[:, :width]
        )
        new_moment = tail[2:3, :] * moment + maps_ref[b, 2 * width : 3 * width, :] - seen[:, width:]
        state = jnp.concatenate([new_memory, new_moment], axis=1)
    refs[0][...] = state


def output_kernel(heads, width, states_ref, high_ref, low_ref, base_ref, out_ref):
    for h in range(heads):
        high, low = halves(states_ref[h])
        read_high = high_ref[h]
        result = base_ref[h] + mul_nt(read_high, high)
        result = result + (mul_nt(read_high, low) + mul_nt(low_ref[h], high))
        out_ref[:, h * width : (h + 1) * width] = result.astype(out_ref.dtype)


def whole(n):
    return [pl.BlockSpec(memory_space=pltpu.VMEM)] * n


def f32(*shape):
    return jax.ShapeDtypeStruct(shape, jnp.float32)


LIMIT = pltpu.CompilerParams(vmem_limit_bytes=48 << 20)


def local(n_outer, n_inner, queries, keys, values, retain, step, momentum, init_memory, init_moment):
    length, heads = retain.shape
    width = init_memory.shape[2]
    axes = ("inner", "outer")
    place = lambda f: (f % n_inner) * n_outer + f // n_inner
    sections = n_outer * n_inner // heads
    teams = [[place(s * heads + j) for j in range(heads)] for s in range(sections)]
    position = lax.axis_index("outer") * n_inner + lax.axis_index("inner")
    section, mine = position // heads, position % heads

    maps = pl.pallas_call(
        functools.partial(map_kernel, heads, width),
        out_shape=f32(heads, 3 * width + TAIL, width),
        in_specs=whole(5),
        out_specs=pl.BlockSpec(memory_space=pltpu.VMEM),
        compiler_params=LIMIT,
    )(keys, values, retain, step, momentum)
    maps = lax.all_to_all(maps, axes, 0, 0, axis_index_groups=teams, tiled=True)

    read_high, read_low, base = pl.pallas_call(
        functools.partial(read_kernel, heads, width),
        out_shape=(
            jax.ShapeDtypeStruct((heads, length, 2 * width), jnp.bfloat16),
            jax.ShapeDtypeStruct((heads, length, 2 * width), jnp.bfloat16),
            f32(heads, length, width),
        ),
        in_specs=whole(6),
        out_specs=tuple(whole(3)),
        compiler_params=LIMIT,
    )(queries, keys, values, retain, step, momentum)

    entry = jnp.concatenate(
        [
            lax.dynamic_index_in_dim(init_memory, mine, 0, keepdims=False),
            lax.dynamic_index_in_dim(init_moment, mine, 0, keepdims=False),
        ],
        axis=1,
    )

    def scan(flag, entry, other, keep_states):
        merged = other is not None
        state = f32(width, 2 * width)
        out = f32(heads, width, 2 * width) if keep_states else (state, state) if merged else state
        given = (entry, other) if merged else (entry,)
        return pl.pallas_call(
            functools.partial(scan_kernel, width, keep_states, merged),
            out_shape=out,
            in_specs=[pl.BlockSpec(memory_space=pltpu.SMEM)] + whole(1 + len(given)),
            out_specs=jax.tree.map(lambda _: pl.BlockSpec(memory_space=pltpu.VMEM), out),
            compiler_params=LIMIT,
        )(flag.astype(jnp.int32).reshape(1), maps, *given)

    other, flag = None, section
    for s in range(sections - 1):
        if s == 0:
            final = scan(flag, entry, None, False)
        else:
            final, entry = scan(flag, entry, other, False)
        other = lax.ppermute(final, axes, list(zip(teams[s], teams[s + 1])))
        flag = section == s + 1
    states = scan(flag, entry, other, True)
    states = lax.all_to_all(states, axes, 0, 0, axis_index_groups=teams, tiled=True)

    return pl.pallas_call(
        functools.partial(output_kernel, heads, width),
        out_shape=jax.ShapeDtypeStruct((length, heads * width), jnp.bfloat16),
        in_specs=whole(4),
        out_specs=pl.BlockSpec(memory_space=pltpu.VMEM),
        compiler_params=LIMIT,
    )(states, read_high, read_low, base)


def solution(mesh):
    rows = P(("groups", "outer", "inner"), None)
    return jax.shard_map(
        functools.partial(local, mesh.shape["outer"], mesh.shape["inner"]),
        mesh=mesh,
        in_specs=(rows,) * 6 + (P(), P()),
        out_specs=rows,
        check_vma=False,
    )
```

time: 609 us -> 98 us (0.16); the launches traced: 601 us -> 97.2 us
  waiting for transfers between devices: 426 us -> 58.4 us
  matrix products: 93.8 us -> 0 us
  local copies, waits for them, and re-layouts: 56.5 us -> 10.9 us
  between operations: 14.2 us -> 0.1 us
  Pallas kernels: 0 us -> 13.7 us
  starting transfers between devices: 0.87 us -> 14.1 us
  other arithmetic: 8.6 us -> 0.01 us
    all_gather x4 -> x0, waiting for transfers between devices: 306 us -> none  [the longest x2 224 us: carried_in(): pieces = jax.tree.map(lambda part: lax.all_gather(part, axis), value)]
    psum x1 -> x0, waiting for transfers between devices: 120 us -> none  [from_root(): return lax.psum(block, axis)]
    dot_general x24 -> x0, matrix products: 93.8 us -> none  [the longest x9 51.8 us: advance_state(): jnp.einsum('hij,hjk->hik', carried, transition, precision=lax.Precision.H...]
    all_to_all x0 -> x2, waiting for transfers between devices: none -> 55.7 us  [the longest x1 36.9 us: local(): maps = lax.all_to_all(maps, axes, 0, 0, axis_index_groups=teams, tiled=True)]
    dynamic_slice x14 -> x0, local copies, waits for them, and re-layouts: 22.2 us -> none  [the longest x6 11.5 us: turn(): longer = join(total, jax.tree.map(lambda part: part[position], pieces))]
    pallas_call x0 -> x5, Pallas kernels: none -> 13.7 us  [the longest x1 4.12 us: local(): pl.pallas_call(functools.partial(read_kernel, heads, width), out_shape=(j...]
    while x19 -> x0, local copies, waits for them, and re-layouts: 11.6 us -> none
    all_to_all x0 -> x2, starting transfers between devices: none -> 11 us  [the longest x1 6.37 us: local(): maps = lax.all_to_all(maps, axes, 0, 0, axis_index_groups=teams, tiled=True)]
  transfers between devices with their start and end apart: 5 -> 3, of which waited for: 5 -> 3; matrix products, arithmetic and copies ran while one was open for 3% -> 1% of each run, Pallas kernels for 0% -> 4%
where the time goes in v1:
time: 98 us; the launch traced here: 97.2 us
  waiting for transfers between devices  58.4 us (60%)
  starting transfers between devices  14.1 us (14%)
  Pallas kernels  13.7 us (14%)
  local copies, waits for them, and re-layouts  10.9 us (11%)
    all_to_all x1, waiting for transfers between devices, local(): maps = lax.all_to_all(maps, axes, 0, 0, axis_index_groups=teams, tiled=True)  36.9 us
    all_to_all x1, waiting for transfers between devices, local(): lax.all_to_all(states, axes, 0, 0, axis_index_groups=teams, tiled=True)  18.8 us
    unnamed x21, local copies, waits for them, and re-layouts  9.99 us
    all_to_all x1, starting transfers between devices, local(): maps = lax.all_to_all(maps, axes, 0, 0, axis_index_groups=teams, tiled=True)  6.37 us
    all_to_all x1, starting transfers between devices, local(): lax.all_to_all(states, axes, 0, 0, axis_index_groups=teams, tiled=True)  4.63 us
    pallas_call x1, Pallas kernels, local(): pl.pallas_call(functools.partial(read_kernel, heads, width), out_shape=(j...  4.12 us
    pallas_call x2, Pallas kernels, scan(): pl.pallas_call(functools.partial(scan_kernel, width, keep_states, merged)...  4.07 us
    pallas_call x1, Pallas kernels, local(): pl.pallas_call(functools.partial(map_kernel, heads, width), out_shape=f32...  3.77 us
  transfers between devices with their start and end apart: 3, of which 3 were waited for; matrix products, arithmetic and copies ran while one was open for 1% of the time, Pallas kernels for 4%

profile of v1, /device:TPU:1, one launch (start us, length us, event | category | flops | bytes accessed | tf_op | source)
XLA Modules:
  0.0 97.2 jit_solution(13870393027308979704)
XLA Ops:
  0.0 0.8 copy.9.retain_ref
  0.8 0.8 copy.10.step_ref
  1.7 0.8 copy.11.momentum_ref
  2.5 0.0 copy-start
  2.5 1.0 %copy-done = bf16[256,1024]{1,0:T(8,128)(2,1)S(1)} copy-done((bf16[256,1024]{1,0:T(8,128)(2,1)S(1)}, bf16[256,1024]{1,0:T(8,128)(2,1)}, u32[]{:S(2)}) %copy-start) | copy-done | bytes 524312
  3.5 1.0 %copy-done.2 = bf16[256,1024]{1,0:T(8,128)(2,1)S(1)} copy-done((bf16[256,1024]{1,0:T(8,128)(2,1)S(1)}, bf16[256,1024]{1,0:T(8,128)(2,1)}, u32[]{:S(2)}) %copy-start.2) | copy-done | bytes 524312
  4.6 3.8 %shard_map.82 = f32[8,392,128]{2,1,0:T(8,128)} custom-call(bf16[256,1024]{1,0:T(8,128)(2,1)S(1)} %copy-done, bf16[256,1024]{1,0:T(8,128)(2,1)S(1)} %copy-done.2, f32[256,8]{1,0:T(8,128)S(1)} %copy.9.retain_ref, f32[256,8]{1,0:T(8,128)S(1)} %copy.10.step_ref, f32[256,8]{1,0:T(8,128)S(1)} %copy.11.momentum_ref), custom_call_target="tpu_custom_call" | custom-call | tf_op jit(solution)/shard_map/pallas_call | solution.py:207
  8.3 6.4 %all-to-all-start = ((f32[8,392,128]{2,1,0:T(8,128)}), f32[8,392,128]{2,1,0:T(8,128)S(1)}, u32[]{:S(2)}, u32[]{:S(2)}) async-start(f32[8,392,128]{2,1,0:T(8,128)} %shard_map.82), calls=%async_computation | async-start | bytes 3211264 | tf_op jit(solution)/shard_map/all_to_all | solution.py:214
  14.7 0.9 dynamic-slice_bitcast_fusion
  15.6 36.9 %all-to-all-done.maps_ref = f32[8,392,128]{2,1,0:T(8,128)S(1)} async-done(((f32[8,392,128]{2,1,0:T(8,128)}), f32[8,392,128]{2,1,0:T(8,128)S(1)}, u32[]{:S(2)}, u32[]{:S(2)}) %all-to-all-start) | async-done | bytes 1605664 | tf_op jit(solution)/shard_map/all_to_all | solution.py:214
  52.6 1.7 %shard_map.83 = f32[128,256]{1,0:T(8,128)S(1)} custom-call(s32[1]{0:T(128)} %bitcast.3.flag_ref, f32[8,392,128]{2,1,0:T(8,128)S(1)} %all-to-all-done.maps_ref, f32[128,256]{1,0:T(8,128)S(1)} %pad_maximum_fusion.entry_ref), custom_call_target="tpu_custom_call" | custom-call | tf_op jit(solution)/shard_map/pallas_call | solution.py:241
  54.2 3.1 %collective-permute-start = (f32[128,256]{1,0:T(8,128)S(1)}, f32[128,256]{1,0:T(8,128)S(1)}, u32[]{:S(2)}, u32[]{:S(2)}) collective-permute-start(f32[128,256]{1,0:T(8,128)S(1)} %shard_map.83), channel_id=1, source_target_pairs={{0,2},{4,6},{8,10},{12,14},{1,3},{5,7},{9,11},{13,15},{16,18},{20,... | collective-permute-start | bytes 393224 | tf_op jit(solution)/shard_map/ppermute | solution.py:255
  57.4 2.7 %collective-permute-done.refs_0_ = f32[128,256]{1,0:T(8,128)S(1)} collective-permute-done((f32[128,256]{1,0:T(8,128)S(1)}, f32[128,256]{1,0:T(8,128)S(1)}, u32[]{:S(2)}, u32[]{:S(2)}) %collective-permute-start) | collective-permute-done | bytes 131104 | tf_op jit(solution)/shard_map/ppermute | solution.py:255
  60.0 2.4 %shard_map.84 = f32[8,128,256]{2,1,0:T(8,128)} custom-call(s32[1]{0:T(128)} %bitcast.flag_ref, f32[8,392,128]{2,1,0:T(8,128)S(1)} %all-to-all-done.maps_ref, f32[128,256]{1,0:T(8,128)S(1)} %pad_maximum_fusion.entry_ref, f32[128,256]{1,0:T(8,128)S(1)} %collective-permute-done.refs_0_), custom_call_target="tpu_custom_call" | custom-call | tf_op jit(solution)/shard_map/pallas_call | solution.py:241
  62.4 4.6 %all-to-all-start.1 = ((f32[8,128,256]{2,1,0:T(8,128)}), f32[8,128,256]{2,1,0:T(8,128)S(1)}, u32[]{:S(2)}, u32[]{:S(2)}) async-start(f32[8,128,256]{2,1,0:T(8,128)} %shard_map.84), calls=%async_computation.1 | async-start | bytes 2097152 | tf_op jit(solution)/shard_map/all_to_all | solution.py:258
  67.1 0.0 copy-start.8
  67.1 1.0 %copy-done.8 = bf16[256,1024]{1,0:T(8,128)(2,1)S(1)} copy-done((bf16[256,1024]{1,0:T(8,128)(2,1)S(1)}, bf16[256,1024]{1,0:T(8,128)(2,1)}, u32[]{:S(2)}) %copy-start.8) | copy-done | bytes 524312
  68.1 4.1 %shard_map.85 = (bf16[8,256,256]{2,1,0:T(8,128)(2,1)S(1)}, bf16[8,256,256]{2,1,0:T(8,128)(2,1)S(1)}, f32[8,256,128]{2,1,0:T(8,128)S(1)}) custom-call(bf16[256,1024]{1,0:T(8,128)(2,1)S(1)} %copy-done.8, bf16[256,1024]{1,0:T(8,128)(2,1)S(1)} %copy-done.1, bf16[256,1024]{1,0:T(8,128)(2,1)S(1)} %copy-done.3, f32[256,8]{1,0:T(8,128)S(1)} %copy.9.retain_ref, ...), custom_call_target="tpu_custom_call" | custom-call | tf_op jit(solution)/shard_map/pallas_call | solution.py:216
  72.3 1.0 %copy-done.4 = bf16[8,256,256]{2,1,0:T(8,128)(2,1)} copy-done((bf16[8,256,256]{2,1,0:T(8,128)(2,1)}, bf16[8,256,256]{2,1,0:T(8,128)(2,1)S(1)}, u32[]{:S(2)}) %copy-start.4) | copy-done | bytes 1048600
  73.2 1.0 copy-done.6
  74.2 18.8 %all-to-all-done.1.states_ref = f32[8,128,256]{2,1,0:T(8,128)S(1)} async-done(((f32[8,128,256]{2,1,0:T(8,128)}), f32[8,128,256]{2,1,0:T(8,128)S(1)}, u32[]{:S(2)}, u32[]{:S(2)}) %all-to-all-start.1) | async-done | bytes 1048608 | tf_op jit(solution)/shard_map/all_to_all | solution.py:258
  93.0 1.2 %copy-done.5 = bf16[8,256,256]{2,1,0:T(8,128)(2,1)S(1)} copy-done((bf16[8,256,256]{2,1,0:T(8,128)(2,1)S(1)}, bf16[8,256,256]{2,1,0:T(8,128)(2,1)}, u32[]{:S(2)}) %copy-start.5) | copy-done | bytes 1048600
  94.2 1.2 %copy-done.7 = f32[8,256,128]{2,1,0:T(8,128)S(1)} copy-done((f32[8,256,128]{2,1,0:T(8,128)S(1)}, f32[8,256,128]{2,1,0:T(8,128)}, u32[]{:S(2)}) %copy-start.7) | copy-done | bytes 1048600
  95.4 1.8 %shard_map.86 = bf16[256,1024]{1,0:T(8,128)(2,1)} custom-call(f32[8,128,256]{2,1,0:T(8,128)S(1)} %all-to-all-done.1.states_ref, bf16[8,256,256]{2,1,0:T(8,128)(2,1)S(1)} %get-tuple-element.8.high_ref, bf16[8,256,256]{2,1,0:T(8,128)(2,1)S(1)} %copy-done.5, f32[8,256,128]{2,1,0:T(8,128)S(1)} %copy-done.7), custom_call_target="tpu_custom_call" | custom-call | tf_op jit(solution)/shard_map/pallas_call | solution.py:260
  (10 shorter events, 0.0 us)
Async XLA Ops:
  2.5 1.0 %copy-start = (bf16[256,1024]{1,0:T(8,128)(2,1)S(1)}, bf16[256,1024]{1,0:T(8,128)(2,1)}, u32[]{:S(2)}) copy-start(bf16[256,1024]{1,0:T(8,128)(2,1)} %k_ref.3) | copy-start | bytes 1572868
  3.5 1.0 %copy-start.2 = (bf16[256,1024]{1,0:T(8,128)(2,1)S(1)}, bf16[256,1024]{1,0:T(8,128)(2,1)}, u32[]{:S(2)}) copy-start(bf16[256,1024]{1,0:T(8,128)(2,1)} %v_ref.3) | copy-start | bytes 1572868
  8.3 44.2 %all-to-all-start = ((f32[8,392,128]{2,1,0:T(8,128)}), f32[8,392,128]{2,1,0:T(8,128)S(1)}, u32[]{:S(2)}, u32[]{:S(2)}) async-start(f32[8,392,128]{2,1,0:T(8,128)} %shard_map.82), calls=%async_computation | async-start | bytes 3211264 | tf_op jit(solution)/shard_map/all_to_all | solution.py:214
  54.2 5.8 %collective-permute-start = (f32[128,256]{1,0:T(8,128)S(1)}, f32[128,256]{1,0:T(8,128)S(1)}, u32[]{:S(2)}, u32[]{:S(2)}) collective-permute-start(f32[128,256]{1,0:T(8,128)S(1)} %shard_map.83), channel_id=1, source_target_pairs={{0,2},{4,6},{8,10},{12,14},{1,3},{5,7},{9,11},{13,15},{16,18},{20,... | collective-permute-start | bytes 393224 | tf_op jit(solution)/shard_map/ppermute | solution.py:255
  62.4 4.6 %copy-start.1 = (bf16[256,1024]{1,0:T(8,128)(2,1)S(1)}, bf16[256,1024]{1,0:T(8,128)(2,1)}, u32[]{:S(2)}) copy-start(bf16[256,1024]{1,0:T(8,128)(2,1)} %k_ref.3) | copy-start | bytes 1572868
  62.4 4.6 %copy-start.3 = (bf16[256,1024]{1,0:T(8,128)(2,1)S(1)}, bf16[256,1024]{1,0:T(8,128)(2,1)}, u32[]{:S(2)}) copy-start(bf16[256,1024]{1,0:T(8,128)(2,1)} %v_ref.3) | copy-start | bytes 1572868
  62.4 30.5 %all-to-all-start.1 = ((f32[8,128,256]{2,1,0:T(8,128)}), f32[8,128,256]{2,1,0:T(8,128)S(1)}, u32[]{:S(2)}, u32[]{:S(2)}) async-start(f32[8,128,256]{2,1,0:T(8,128)} %shard_map.84), calls=%async_computation.1 | async-start | bytes 2097152 | tf_op jit(solution)/shard_map/all_to_all | solution.py:258
  67.1 1.0 %copy-start.8 = (bf16[256,1024]{1,0:T(8,128)(2,1)S(1)}, bf16[256,1024]{1,0:T(8,128)(2,1)}, u32[]{:S(2)}) copy-start(bf16[256,1024]{1,0:T(8,128)(2,1)} %q_ref.1) | copy-start | bytes 1572868
  72.3 1.0 %copy-start.4 = (bf16[8,256,256]{2,1,0:T(8,128)(2,1)}, bf16[8,256,256]{2,1,0:T(8,128)(2,1)S(1)}, u32[]{:S(2)}) copy-start(bf16[8,256,256]{2,1,0:T(8,128)(2,1)S(1)} %get-tuple-element.9.low_ref) | copy-start | bytes 3145732
  73.2 1.0 copy-start.6
  93.0 1.2 %copy-start.5 = (bf16[8,256,256]{2,1,0:T(8,128)(2,1)S(1)}, bf16[8,256,256]{2,1,0:T(8,128)(2,1)}, u32[]{:S(2)}) copy-start(bf16[8,256,256]{2,1,0:T(8,128)(2,1)} %copy-done.4) | copy-start | bytes 3145732
  94.2 1.2 %copy-start.7 = (f32[8,256,128]{2,1,0:T(8,128)S(1)}, f32[8,256,128]{2,1,0:T(8,128)}, u32[]{:S(2)}) copy-start(f32[8,256,128]{2,1,0:T(8,128)} %copy-done.6) | copy-start | bytes 3145732

commit v2 on v1

v2 whole, which is shorter than its diff:
```python
import functools

import jax
import jax.numpy as jnp
from jax import lax
from jax.experimental import pallas as pl
from jax.experimental.pallas import tpu as pltpu
from jax.sharding import PartitionSpec as P

CHUNKS = 1
TAIL = 8
EPS = 1e-06
EXACT = lax.Precision.HIGHEST


def halves(x):
    high = x.astype(jnp.bfloat16)
    return high, (x - high.astype(jnp.float32)).astype(jnp.bfloat16)


def mul(a, b, dims):
    return lax.dot_general(a, b, (dims, ((), ())), preferred_element_type=jnp.float32)


def mul_tn(a, b):
    return mul(a, b, ((0,), (0,)))


def mul_nt(a, b):
    return mul(a, b, ((1,), (1,)))


def mul_nn(a, b):
    return mul(a, b, ((1,), (0,)))


def exact(a, b):
    return jnp.dot(a, b, precision=EXACT, preferred_element_type=jnp.float32)


def grid_ids(shape):
    return lax.broadcasted_iota(jnp.int32, shape, 0), lax.broadcasted_iota(jnp.int32, shape, 1)


def fetch(sources, targets, sem):
    copies = [
        pltpu.make_async_copy(s, t, sem.at[n]) for n, (s, t) in enumerate(zip(sources, targets))
    ]
    for copy in copies:
        copy.start()
    return copies


def map_kernel(heads, width, chunks, mine_ref, *refs):
    hbm = refs[:5]
    outs = refs[5 : 5 + chunks * heads]
    k_ref, v_ref, retain_ref, step_ref, momentum_ref, *made, in_sem = refs[5 + chunks * heads :]
    rows = width // chunks
    copies = fetch(hbm, (k_ref, v_ref, retain_ref, step_ref, momentum_ref), in_sem)
    length = k_ref.shape[0]
    row, col = grid_ids((length, length))
    before = (row <= col).astype(jnp.float32)
    after = (row >= col).astype(jnp.float32)
    drow, dcol = grid_ids((width, width))
    keep = drow <= dcol
    diagonal = drow == dcol
    for copy in copies[2:]:
        copy.wait()
    step = step_ref[...]
    logs = exact(jnp.concatenate([jnp.log(retain_ref[...]), jnp.log(momentum_ref[...])], axis=0), before)
    log_retain, log_moment = logs[:heads], logs[heads:]
    decay = jnp.exp(log_moment)
    reach = jnp.exp(log_retain[:, length - 1 :] - log_retain) * decay
    suffix = exact(reach, after)
    memory_weight = (suffix / decay * step).T
    moment_weight = (jnp.exp(log_moment[:, length - 1 :] - log_moment) * step).T
    retain_end = jnp.exp(log_retain[:, length - 1 :])
    moment_end = decay[:, length - 1 :]
    carry_end = suffix[:, :1]
    for copy in copies[:2]:
        copy.wait()
    for h in range(heads):
        lanes = slice(h * width, (h + 1) * width)
        keys = k_ref[:, lanes]
        values = v_ref[:, lanes]
        wide = keys.astype(jnp.float32)
        scale = lax.rsqrt(jnp.sum(wide * wide, -1, keepdims=True) + EPS)
        weight_m = memory_weight[:, h : h + 1] * scale
        weight_s = moment_weight[:, h : h + 1] * scale
        write = jnp.concatenate([wide * weight_m, wide * weight_s], axis=1)
        high, low = halves(write)
        offset = mul_tn(values, high) + mul_tn(values, low)
        high, low = halves(write * scale)
        gram = mul_tn(keys, high) + mul_tn(keys, low)
        moment_gram = gram[:, width:]
        on_diagonal = jnp.sum(jnp.where(diagonal, moment_gram, 0.0), axis=0, keepdims=True)
        wide_row = lambda x: jnp.broadcast_to(x[h : h + 1, :], (1, width))
        made[0][h, :width, :] = jnp.where(keep, gram[:, :width], moment_gram)
        made[0][h, width : width + TAIL, :] = jnp.concatenate(
            [
                on_diagonal,
                wide_row(retain_end),
                wide_row(moment_end),
                wide_row(carry_end),
                jnp.zeros((TAIL - 4, width), jnp.float32),
            ],
            axis=0,
        )
        for c in range(chunks):
            at = width + TAIL if c == 0 else 0
            part = offset[c * rows : (c + 1) * rows]
            made[c][h, at : at + rows, :] = part[:, :width]
            made[c][h, at + rows : at + 2 * rows, :] = part[:, width:]
    mine = mine_ref[0]
    for c in range(chunks):
        for s in range(heads):
            outs[c * heads + s][...] = made[c][lax.rem(mine + s, heads)]


def read_kernel(
    heads, width, q_ref, k_ref, v_ref, retain_ref, step_ref, momentum_ref, high_ref, low_ref, base_ref
):
    length = k_ref.shape[0]
    row, col = grid_ids((length, length))
    before = (row <= col).astype(jnp.float32)
    causal = row >= col
    lower = causal.astype(jnp.bfloat16)
    logs = exact(jnp.concatenate([jnp.log(retain_ref[...]), jnp.log(momentum_ref[...])], axis=0), before)
    log_retain, log_moment = logs[:heads], logs[heads:]
    log_gap = log_moment - log_retain
    step_rows = step_ref[...] * jnp.exp(-log_moment)
    log_column = log_retain.T
    retain_scale = jnp.exp(log_column)
    ones = jnp.ones((8, width), jnp.bfloat16)
    for h in range(heads):
        lanes = slice(h * width, (h + 1) * width)
        queries, keys, values = q_ref[:, lanes], k_ref[:, lanes], v_ref[:, lanes]
        wide_q = queries.astype(jnp.float32)
        wide_k = keys.astype(jnp.float32)
        query_scale = lax.rsqrt(jnp.sum(wide_q * wide_q, -1, keepdims=True) + EPS)
        high, low = halves(wide_k * wide_k)
        key_scale = lax.rsqrt((mul_nt(ones, high) + mul_nt(ones, low))[:1, :] + EPS)
        gap = log_column[:, h : h + 1] + log_gap[h : h + 1, :]
        reach = jnp.exp(jnp.where(causal, gap, -1e30))
        high, low = halves(reach)
        weights = mul_nn(high, lower) + mul_nn(low, lower)
        mixing = mul_nt(queries, keys) * weights * (step_rows[h : h + 1, :] * key_scale)
        high, low = halves(mixing)
        base_ref[h] = query_scale * (mul_nn(high, values) + mul_nn(low, values))
        high, low = halves(mixing * key_scale)
        seen = mul_nn(high, keys) + mul_nn(low, keys)
        unit_q = query_scale * wide_q
        reads = jnp.concatenate(
            [retain_scale[:, h : h + 1] * unit_q - query_scale * seen, weights[:, :1] * unit_q], axis=1
        )
        high, low = halves(reads)
        high_ref[h] = high
        low_ref[h] = low


def scan_kernel(heads, width, chunk, chunks, keep_states, merged, scalar_ref, entry_ref, *refs):
    rows = width // chunks
    here = slice(chunk * rows, (chunk + 1) * rows) if entry_ref.shape[0] == width else slice(0, rows)
    entry = entry_ref[here]
    if merged:
        other_ref, *refs = refs
        entry = jnp.where(scalar_ref[1] > 0, other_ref[...], entry)
    given = heads if chunk == 0 else 2 * heads
    arrived, refs = refs[:given], refs[given:]
    outs, refs = (refs[:heads], refs[heads:]) if keep_states else (refs[: 1 + merged], refs[1 + merged :])
    first_ref = refs[0]
    offset_ref = refs[1] if chunk > 0 else first_ref
    mine = scalar_ref[0]
    for n, ref in enumerate(arrived):
        target = first_ref if n < heads else offset_ref
        target[lax.rem(mine + heads - n % heads, heads)] = ref[...]
    row, col = grid_ids((width, width))
    at = 0 if chunk > 0 else width + TAIL
    if not keep_states and merged:
        outs[1][...] = entry
    if keep_states:
        states_ref = refs[-1]
    state = entry
    for b in range(heads):
        if keep_states:
            states_ref[b] = state
            if b == heads - 1:
                break
        packed = first_ref[b, :width, :]
        flipped = packed.T
        tail = first_ref[b, width : width + TAIL, :]
        gram = jnp.concatenate(
            [
                jnp.where(row <= col, packed, flipped),
                jnp.where(row == col, tail[:1, :], jnp.where(row > col, packed, flipped)),
            ],
            axis=1,
        )
        gram_high, gram_low = halves(gram)
        memory, moment = state[:, :width], state[:, width:]
        high, low = halves(memory)
        seen = mul_nn(high, gram_high) + (mul_nn(high, gram_low) + mul_nn(low, gram_high))
        new_memory = (
            tail[1:2, :] * memory + tail[3:4, :] * moment + offset_ref[b, at : at + rows, :] - seen[:, :width]
        )
        new_moment = tail[2:3, :] * moment + offset_ref[b, at + rows : at + 2 * rows, :] - seen[:, width:]
        state = jnp.concatenate([new_memory, new_moment], axis=1)
    if not keep_states:
        outs[0][...] = state
        return
    for s in range(heads):
        outs[s][...] = states_ref[lax.rem(mine + s, heads)]


def output_kernel(heads, width, chunks, mine_ref, *refs):
    arrived, refs = refs[: heads * chunks], refs[heads * chunks :]
    read_high_ref, read_low_ref, base_ref, out_ref = refs
    mine = mine_ref[0]
    for s in range(heads):
        h = lax.rem(mine + heads - s, heads)
        high, low = halves(jnp.concatenate([arrived[c * heads + s][...] for c in range(chunks)], axis=0))
        read_high = read_high_ref[h]
        result = base_ref[h] + mul_nt(read_high, high)
        result = result + (mul_nt(read_high, low) + mul_nt(read_low_ref[h], high))
        lanes = pl.ds(pl.multiple_of(h * width, width), width)
        out_ref[:, lanes] = result.astype(out_ref.dtype)


VMEM = pl.BlockSpec(memory_space=pltpu.VMEM)
HBM = pl.BlockSpec(memory_space=pltpu.HBM)
SMEM = pl.BlockSpec(memory_space=pltpu.SMEM)
LIMIT = pltpu.CompilerParams(vmem_limit_bytes=24 << 20)
DMA = pltpu.SemaphoreType.DMA


def f32(*shape):
    return jax.ShapeDtypeStruct(shape, jnp.float32)


def local(n_outer, n_inner, queries, keys, values, retain, step, momentum, init_memory, init_moment):
    length, heads = retain.shape
    width = init_memory.shape[2]
    chunks = CHUNKS
    rows = width // chunks
    axes = ("inner", "outer")
    place = lambda f: (f % n_inner) * n_outer + f // n_inner
    sections = n_outer * n_inner // heads
    teams = [[place(s * heads + j) for j in range(heads)] for s in range(sections)]
    position = lax.axis_index("outer") * n_inner + lax.axis_index("inner")
    section, mine = position // heads, position % heads
    scalars = lambda *xs: jnp.stack([jnp.asarray(x).astype(jnp.int32) for x in xs])
    gates = (retain.T, step.T, momentum.T)

    def swap(pieces):
        moved = [pieces[0]]
        for s in range(1, heads):
            pairs = [(team[j], team[(j + s) % heads]) for team in teams for j in range(heads)]
            moved.append(lax.ppermute(pieces[s], axes, pairs))
        return moved

    shapes = [(width + TAIL + 2 * rows, width)] + [(2 * rows, width)] * (chunks - 1)
    made = pl.pallas_call(
        functools.partial(map_kernel, heads, width, chunks),
        out_shape=[f32(*shape) for shape in shapes for _ in range(heads)],
        in_specs=[SMEM] + [HBM] * 5,
        out_specs=[VMEM] * (chunks * heads),
        scratch_shapes=[pltpu.VMEM(keys.shape, keys.dtype)] * 2
        + [pltpu.VMEM((heads, length), jnp.float32)] * 3
        + [pltpu.VMEM((heads, *shape), jnp.float32) for shape in shapes]
        + [DMA((5,))],
        compiler_params=LIMIT,
    )(scalars(mine), keys, values, *gates)
    maps = [swap(made[c * heads : (c + 1) * heads]) for c in range(chunks)]

    read_high, read_low, base = pl.pallas_call(
        functools.partial(read_kernel, heads, width),
        out_shape=(
            jax.ShapeDtypeStruct((heads, length, 2 * width), jnp.bfloat16),
            jax.ShapeDtypeStruct((heads, length, 2 * width), jnp.bfloat16),
            f32(heads, length, width),
        ),
        in_specs=[VMEM] * 6,
        out_specs=(VMEM,) * 3,
        compiler_params=LIMIT,
    )(queries, keys, values, *gates)

    start = jnp.concatenate(
        [
            lax.dynamic_index_in_dim(init_memory, mine, 0, keepdims=False),
            lax.dynamic_index_in_dim(init_moment, mine, 0, keepdims=False),
        ],
        axis=1,
    )

    def scan(c, flag, entry, other, keep_states):
        merged = other is not None
        state = f32(rows, 2 * width)
        out = [state] * (heads if keep_states else 1 + merged)
        given = ([other] if merged else []) + maps[0] + (maps[c] if c > 0 else [])
        scratch = [pltpu.VMEM((heads, *shapes[0]), jnp.float32)]
        if c > 0:
            scratch.append(pltpu.VMEM((heads, *shapes[c]), jnp.float32))
        if keep_states:
            scratch.append(pltpu.VMEM((heads, rows, 2 * width), jnp.float32))
        return pl.pallas_call(
            functools.partial(scan_kernel, heads, width, c, chunks, keep_states, merged),
            out_shape=out,
            in_specs=[SMEM, VMEM] + [VMEM] * len(given),
            out_specs=[VMEM] * len(out),
            scratch_shapes=scratch,
            compiler_params=LIMIT,
        )(scalars(mine, flag), entry, *given)

    states = []
    for c in range(chunks):
        entry, other, flag = start, None, section
        for s in range(sections - 1):
            final, *kept = scan(c, flag, entry, other, False)
            if kept:
                entry = kept[0]
            other = lax.ppermute(final, axes, list(zip(teams[s], teams[s + 1])))
            flag = section == s + 1
        states += swap(scan(c, flag, entry, other, True))

    return pl.pallas_call(
        functools.partial(output_kernel, heads, width, chunks),
        out_shape=jax.ShapeDtypeStruct((length, heads * width), jnp.bfloat16),
        in_specs=[SMEM] + [VMEM] * (heads * chunks + 3),
        out_specs=VMEM,
        compiler_params=LIMIT,
    )(scalars(mine), *states, read_high, read_low, base)


def solution(mesh):
    rows = P(("groups", "outer", "inner"), None)
    return jax.shard_map(
        functools.partial(local, mesh.shape["outer"], mesh.shape["inner"]),
        mesh=mesh,
        in_specs=(rows,) * 6 + (P(), P()),
        out_specs=rows,
        check_vma=False,
    )
```

time: 98 us -> 83.7 us (0.85)
  waiting for transfers between devices: 58.4 us -> 8.87 us
  starting transfers between devices: 14.1 us -> 56.9 us
  local copies, waits for them, and re-layouts: 10.9 us -> 3.69 us
    all_to_all x2 -> x0, waiting for transfers between devices: 55.7 us -> none  [the longest x1 36.9 us: local(): maps = lax.all_to_all(maps, axes, 0, 0, axis_index_groups=teams, tiled=True)]
    ppermute x0 -> x14, starting transfers between devices: none -> 53.2 us  [swap(): moved.append(lax.ppermute(pieces[s], axes, pairs))]
    all_to_all x2 -> x0, starting transfers between devices: 11 us -> none  [the longest x1 6.37 us: local(): maps = lax.all_to_all(maps, axes, 0, 0, axis_index_groups=teams, tiled=True)]
    unnamed x21 -> x16, local copies, waits for them, and re-layouts: 9.99 us -> 2.81 us
    ppermute x0 -> x14, waiting for transfers between devices: none -> 7.03 us  [swap(): moved.append(lax.ppermute(pieces[s], axes, pairs))]
  transfers between devices with their start and end apart: 3 -> 15, of which waited for: 3 -> 4; matrix products, arithmetic and copies ran while one was open for 1% -> 1% of each run, Pallas kernels for 4% -> 5%
where the time goes in v2:
time: 83.7 us; the launch traced here: 83.2 us
  starting transfers between devices  56.9 us (68%)
  Pallas kernels  13.5 us (16%)
  waiting for transfers between devices  8.87 us (11%)
  local copies, waits for them, and re-layouts  3.69 us (4%)
    ppermute x14, starting transfers between devices, swap(): moved.append(lax.ppermute(pieces[s], axes, pairs))  53.2 us
    ppermute x14, waiting for transfers between devices, swap(): moved.append(lax.ppermute(pieces[s], axes, pairs))  7.03 us
    pallas_call x2, Pallas kernels, scan(): pl.pallas_call(functools.partial(scan_kernel, heads, width, c, chunks, ke...  4.47 us
    pallas_call x1, Pallas kernels, local(): pl.pallas_call(functools.partial(read_kernel, heads, width), out_shape=(j...  3.78 us
    ppermute x1, starting transfers between devices, local(): other = lax.ppermute(final, axes, list(zip(teams[s], teams[s + 1])))  3.66 us
    pallas_call x1, Pallas kernels, local(): pl.pallas_call(functools.partial(map_kernel, heads, width, chunks), out_s...  3.36 us
    unnamed x16, local copies, waits for them, and re-layouts  2.81 us
    pallas_call x1, Pallas kernels, local(): pl.pallas_call(functools.partial(output_kernel, heads, width, chunks), ou...  1.87 us
  transfers between devices with their start and end apart: 15, of which 4 were waited for; matrix products, arithmetic and copies ran while one was open for 1% of the time, Pallas kernels for 5%

profile of v2, /device:TPU:1, one launch (start us, length us, event | category | flops | bytes accessed | tf_op | source)
XLA Modules:
  0.0 83.2 jit_solution(1948080440813169074)
XLA Ops:
  0.7 1.0 %copy-done = bf16[256,1024]{1,0:T(8,128)(2,1)S(1)} copy-done((bf16[256,1024]{1,0:T(8,128)(2,1)S(1)}, bf16[256,1024]{1,0:T(8,128)(2,1)}, u32[]{:S(2)}) %copy-start) | copy-done | bytes 524312
  1.8 1.0 %copy-done.2 = bf16[256,1024]{1,0:T(8,128)(2,1)S(1)} copy-done((bf16[256,1024]{1,0:T(8,128)(2,1)S(1)}, bf16[256,1024]{1,0:T(8,128)(2,1)}, u32[]{:S(2)}) %copy-start.2) | copy-done | bytes 524312
  2.8 3.4 %shard_map.82 = (f32[392,128]{1,0:T(8,128)S(1)}, f32[392,128]{1,0:T(8,128)S(1)}, f32[392,128]{1,0:T(8,128)S(1)}, f32[392,128]{1,0:T(8,128)S(1)}, f32[392,128]{1,...) custom-call(s32[1]{0:T(128)} %bitcast.mine_ref, ...), custom_call_target="tpu_custom_call" | custom-call | tf_op jit(solution)/shard_map/pallas_call | solution.py:262
  6.2 2.2 %collective-permute-start = (f32[392,128]{1,0:T(8,128)S(1)}, f32[392,128]{1,0:T(8,128)S(1)}, u32[]{:S(2)}, u32[]{:S(2)}) collective-permute-start(f32[392,128]{1,0:T(8,128)S(1)} %get-tuple-element.25), channel_id=1, source_target_pairs={{0,4},{4,8},{8,12},{12,1},{1,5},{5,9},{9,13},{13,0},{2,6},{6,10},{... | collective-permute-start | bytes 602120 | tf_op jit(solution)/shard_map/ppermute | solution.py:258
  8.4 2.3 %collective-permute-start.1 = (f32[392,128]{1,0:T(8,128)S(1)}, f32[392,128]{1,0:T(8,128)S(1)}, u32[]{:S(2)}, u32[]{:S(2)}) collective-permute-start(f32[392,128]{1,0:T(8,128)S(1)} %get-tuple-element.26), channel_id=1, source_target_pairs={{0,8},{4,12},{8,1},{12,5},{1,9},{5,13},{9,0},{13,4},{2,10},{6,14},... | collective-permute-start | bytes 602120 | tf_op jit(solution)/shard_map/ppermute | solution.py:258
  10.7 1.9 %collective-permute-start.2 = (f32[392,128]{1,0:T(8,128)S(1)}, f32[392,128]{1,0:T(8,128)S(1)}, u32[]{:S(2)}, u32[]{:S(2)}) collective-permute-start(f32[392,128]{1,0:T(8,128)S(1)} %get-tuple-element.27), channel_id=1, source_target_pairs={{0,12},{4,1},{8,5},{12,9},{1,13},{5,0},{9,4},{13,8},{2,14},{6,3},{... | collective-permute-start | bytes 602120 | tf_op jit(solution)/shard_map/ppermute | solution.py:258
  12.6 1.1 %collective-permute-start.4 = (f32[392,128]{1,0:T(8,128)S(1)}, f32[392,128]{1,0:T(8,128)S(1)}, u32[]{:S(2)}, u32[]{:S(2)}) collective-permute-start(f32[392,128]{1,0:T(8,128)S(1)} %get-tuple-element.29), channel_id=1, source_target_pairs={{0,5},{4,9},{8,13},{12,0},{1,4},{5,8},{9,12},{13,1},{2,7},{6,11},{... | collective-permute-start | bytes 602120 | tf_op jit(solution)/shard_map/ppermute | solution.py:258
  13.7 0.9 %dynamic-slice_bitcast_fusion = (f32[128,128]{1,0:T(8,128)S(1)}, f32[128,128]{1,0:T(8,128)S(1)}) fusion(f32[8,128,128]{2,1,0:T(8,128)} %param.15, s32[]{:T(128)S(6)} %select_n.18, f32[8,128,128]{2,1,0:T(8,128)} %param.14), kind=kLoop, calls=%fused_computation.1 | loop fusion | bytes 262148 | tf_op jit(solution)/shard_map/jit(dynamic_index_in_dim)/squeeze | solution.py:290
  14.5 2.0 %collective-permute-done.refs_1_.refs_2_ = f32[392,128]{1,0:T(8,128)S(1)} collective-permute-done((f32[392,128]{1,0:T(8,128)S(1)}, f32[392,128]{1,0:T(8,128)S(1)}, u32[]{:S(2)}, u32[]{:S(2)}) %collective-permute-start) | collective-permute-done | bytes 200736 | tf_op jit(solution)/shard_map/ppermute | solution.py:258
  16.6 9.9 %collective-permute-start.5 = (f32[392,128]{1,0:T(8,128)S(1)}, f32[392,128]{1,0:T(8,128)S(1)}, u32[]{:S(2)}, u32[]{:S(2)}) collective-permute-start(f32[392,128]{1,0:T(8,128)S(1)} %get-tuple-element.30), channel_id=1, source_target_pairs={{0,9},{4,13},{8,0},{12,4},{1,8},{5,12},{9,1},{13,5},{2,11},{6,15},... | collective-permute-start | bytes 602120 | tf_op jit(solution)/shard_map/ppermute | solution.py:258
  26.5 11.6 %collective-permute-start.6 = (f32[392,128]{1,0:T(8,128)S(1)}, f32[392,128]{1,0:T(8,128)S(1)}, u32[]{:S(2)}, u32[]{:S(2)}) collective-permute-start(f32[392,128]{1,0:T(8,128)S(1)} %get-tuple-element.31), channel_id=1, source_target_pairs={{0,13},{4,0},{8,4},{12,8},{1,12},{5,1},{9,5},{13,9},{2,15},{6,2},{... | collective-permute-start | bytes 602120 | tf_op jit(solution)/shard_map/ppermute | solution.py:258
  38.2 3.5 %collective-permute-done.5.refs_6_.refs_7_ = f32[392,128]{1,0:T(8,128)S(1)} collective-permute-done((f32[392,128]{1,0:T(8,128)S(1)}, f32[392,128]{1,0:T(8,128)S(1)}, u32[]{:S(2)}, u32[]{:S(2)}) %collective-permute-start.5) | collective-permute-done | bytes 200736 | tf_op jit(solution)/shard_map/ppermute | solution.py:258
  41.8 2.3 %shard_map.83 = f32[128,256]{1,0:T(8,128)S(1)} custom-call(s32[2]{0:T(128)S(1)} %pad_add_fusion.1.scalar_ref, f32[128,256]{1,0:T(8,128)S(1)} %pad_maximum_fusion.entry_ref, f32[392,128]{1,0:T(8,128)S(1)} %get-tuple-element.24.refs_0_.refs_1_, f32[392,128]{1,0:T(8,128)S(1)} %collective-permute-done.refs_1_.refs_2_, ...), custom_call_target="tpu_custom_call" | custom-call | tf_op jit(solution)/shard_map/pallas_call | solution.py:305
  44.1 3.7 %collective-permute-start.7 = (f32[128,256]{1,0:T(8,128)S(1)}, f32[128,256]{1,0:T(8,128)S(1)}, u32[]{:S(2)}, u32[]{:S(2)}) collective-permute-start(f32[128,256]{1,0:T(8,128)S(1)} %shard_map.83), channel_id=1, source_target_pairs={{0,2},{4,6},{8,10},{12,14},{1,3},{5,7},{9,11},{13,15},{16,18},{20,... | collective-permute-start | bytes 393224 | tf_op jit(solution)/shard_map/ppermute | solution.py:321
  47.8 1.8 %collective-permute-done.7.refs_0_ = f32[128,256]{1,0:T(8,128)S(1)} collective-permute-done((f32[128,256]{1,0:T(8,128)S(1)}, f32[128,256]{1,0:T(8,128)S(1)}, u32[]{:S(2)}, u32[]{:S(2)}) %collective-permute-start.7) | collective-permute-done | bytes 131104 | tf_op jit(solution)/shard_map/ppermute | solution.py:321
  49.7 2.2 %shard_map.84 = (f32[128,256]{1,0:T(8,128)S(1)}, f32[128,256]{1,0:T(8,128)S(1)}, f32[128,256]{1,0:T(8,128)S(1)}, f32[128,256]{1,0:T(8,128)S(1)}, f32[128,256]{1,...) custom-call(s32[2]{0:T(128)S(1)} %pad_add_fusion.scalar_ref, ...), custom_call_target="tpu_custom_call" | custom-call | tf_op jit(solution)/shard_map/pallas_call | solution.py:305
  51.8 5.2 %collective-permute-start.8 = (f32[128,256]{1,0:T(8,128)S(1)}, f32[128,256]{1,0:T(8,128)S(1)}, u32[]{:S(2)}, u32[]{:S(2)}) collective-permute-start(f32[128,256]{1,0:T(8,128)S(1)} %get-tuple-element.33), channel_id=1, source_target_pairs={{0,4},{4,8},{8,12},{12,1},{1,5},{5,9},{9,13},{13,0},{2,6},{6,10},{... | collective-permute-start | bytes 393224 | tf_op jit(solution)/shard_map/ppermute | solution.py:258
  57.0 1.4 %collective-permute-start.9 = (f32[128,256]{1,0:T(8,128)S(1)}, f32[128,256]{1,0:T(8,128)S(1)}, u32[]{:S(2)}, u32[]{:S(2)}) collective-permute-start(f32[128,256]{1,0:T(8,128)S(1)} %get-tuple-element.34), channel_id=1, source_target_pairs={{0,8},{4,12},{8,1},{12,5},{1,9},{5,13},{9,0},{13,4},{2,10},{6,14},... | collective-permute-start | bytes 393224 | tf_op jit(solution)/shard_map/ppermute | solution.py:258
  58.4 1.9 %collective-permute-start.10 = (f32[128,256]{1,0:T(8,128)S(1)}, f32[128,256]{1,0:T(8,128)S(1)}, u32[]{:S(2)}, u32[]{:S(2)}) collective-permute-start(f32[128,256]{1,0:T(8,128)S(1)} %get-tuple-element.35), channel_id=1, source_target_pairs={{0,12},{4,1},{8,5},{12,9},{1,13},{5,0},{9,4},{13,8},{2,14},{6,3},{... | collective-permute-start | bytes 393224 | tf_op jit(solution)/shard_map/ppermute | solution.py:258
  61.1 1.4 %collective-permute-done.8.refs_1_ = f32[128,256]{1,0:T(8,128)S(1)} collective-permute-done((f32[128,256]{1,0:T(8,128)S(1)}, f32[128,256]{1,0:T(8,128)S(1)}, u32[]{:S(2)}, u32[]{:S(2)}) %collective-permute-start.8) | collective-permute-done | bytes 131104 | tf_op jit(solution)/shard_map/ppermute | solution.py:258
  62.5 5.6 %collective-permute-start.13 = (f32[128,256]{1,0:T(8,128)S(1)}, f32[128,256]{1,0:T(8,128)S(1)}, u32[]{:S(2)}, u32[]{:S(2)}) collective-permute-start(f32[128,256]{1,0:T(8,128)S(1)} %get-tuple-element.38), channel_id=1, source_target_pairs={{0,9},{4,13},{8,0},{12,4},{1,8},{5,12},{9,1},{13,5},{2,11},{6,15},... | collective-permute-start | bytes 393224 | tf_op jit(solution)/shard_map/ppermute | solution.py:258
  68.1 9.4 %collective-permute-start.14 = (f32[128,256]{1,0:T(8,128)S(1)}, f32[128,256]{1,0:T(8,128)S(1)}, u32[]{:S(2)}, u32[]{:S(2)}) collective-permute-start(f32[128,256]{1,0:T(8,128)S(1)} %get-tuple-element.39), channel_id=1, source_target_pairs={{0,13},{4,0},{8,4},{12,8},{1,12},{5,1},{9,5},{13,9},{2,15},{6,2},{... | collective-permute-start | bytes 393224 | tf_op jit(solution)/shard_map/ppermute | solution.py:258
  77.5 3.8 %shard_map.85 = (bf16[8,256,256]{2,1,0:T(8,128)(2,1)S(1)}, bf16[8,256,256]{2,1,0:T(8,128)(2,1)S(1)}, f32[8,256,128]{2,1,0:T(8,128)S(1)}) custom-call(bf16[256,1024]{1,0:T(8,128)(2,1)S(1)} %copy-done.4, bf16[256,1024]{1,0:T(8,128)(2,1)S(1)} %copy-done.1, bf16[256,1024]{1,0:T(8,128)(2,1)S(1)} %copy-done.3, f32[8,256]{1,0:T(8,128)S(1)} %bitcast.11, ...), custom_call_target="tpu_custom_call" | custom-call | tf_op jit(solution)/shard_map/pallas_call | solution.py:275
  81.3 1.9 %shard_map.86 = bf16[256,1024]{1,0:T(8,128)(2,1)} custom-call(s32[1]{0:T(128)} %bitcast.mine_ref, f32[128,256]{1,0:T(8,128)S(1)} %get-tuple-element.32.refs_0_, f32[128,256]{1,0:T(8,128)S(1)} %collective-permute-done.8.refs_1_, f32[128,256]{1,0:T(8,128)S(1)} %collective-permute-done.9.refs_2_, f32[128,256]{1,0:T(8,128)S(1)} %collective-permute-done.10.refs_3_, ...), custom_call_target="tpu_custom_call" | custom-call | tf_op jit(solution)/shard_map/pallas_call | solution.py:325
  (31 shorter events, 1.8 us)
Async XLA Ops:
  0.0 0.7 copy-start.7
  0.0 0.7 copy-start.6
  0.0 0.7 copy-start.5
  0.7 1.0 %copy-start = (bf16[256,1024]{1,0:T(8,128)(2,1)S(1)}, bf16[256,1024]{1,0:T(8,128)(2,1)}, u32[]{:S(2)}) copy-start(bf16[256,1024]{1,0:T(8,128)(2,1)} %k_ref.1) | copy-start | bytes 1572868
  1.8 1.0 %copy-start.2 = (bf16[256,1024]{1,0:T(8,128)(2,1)S(1)}, bf16[256,1024]{1,0:T(8,128)(2,1)}, u32[]{:S(2)}) copy-start(bf16[256,1024]{1,0:T(8,128)(2,1)} %v_ref.1) | copy-start | bytes 1572868
  6.2 10.4 %collective-permute-start = (f32[392,128]{1,0:T(8,128)S(1)}, f32[392,128]{1,0:T(8,128)S(1)}, u32[]{:S(2)}, u32[]{:S(2)}) collective-permute-start(f32[392,128]{1,0:T(8,128)S(1)} %get-tuple-element.25), channel_id=1, source_target_pairs={{0,4},{4,8},{8,12},{12,1},{1,5},{5,9},{9,13},{13,0},{2,6},{6,10},{... | collective-permute-start | bytes 602120 | tf_op jit(solution)/shard_map/ppermute | solution.py:258
  8.4 18.1 %collective-permute-start.1 = (f32[392,128]{1,0:T(8,128)S(1)}, f32[392,128]{1,0:T(8,128)S(1)}, u32[]{:S(2)}, u32[]{:S(2)}) collective-permute-start(f32[392,128]{1,0:T(8,128)S(1)} %get-tuple-element.26), channel_id=1, source_target_pairs={{0,8},{4,12},{8,1},{12,5},{1,9},{5,13},{9,0},{13,4},{2,10},{6,14},... | collective-permute-start | bytes 602120 | tf_op jit(solution)/shard_map/ppermute | solution.py:258
  10.7 27.5 %collective-permute-start.2 = (f32[392,128]{1,0:T(8,128)S(1)}, f32[392,128]{1,0:T(8,128)S(1)}, u32[]{:S(2)}, u32[]{:S(2)}) collective-permute-start(f32[392,128]{1,0:T(8,128)S(1)} %get-tuple-element.27), channel_id=1, source_target_pairs={{0,12},{4,1},{8,5},{12,9},{1,13},{5,0},{9,4},{13,8},{2,14},{6,3},{... | collective-permute-start | bytes 602120 | tf_op jit(solution)/shard_map/ppermute | solution.py:258
  12.6 25.6 %collective-permute-start.3 = (f32[392,128]{1,0:T(8,128)S(1)}, f32[392,128]{1,0:T(8,128)S(1)}, u32[]{:S(2)}, u32[]{:S(2)}) collective-permute-start(f32[392,128]{1,0:T(8,128)S(1)} %get-tuple-element.28), channel_id=1, source_target_pairs={{0,1},{4,5},{8,9},{12,13},{1,0},{5,4},{9,8},{13,12},{2,3},{6,7},{1... | collective-permute-start | bytes 602120 | tf_op jit(solution)/shard_map/ppermute | solution.py:258
  12.6 25.6 %collective-permute-start.4 = (f32[392,128]{1,0:T(8,128)S(1)}, f32[392,128]{1,0:T(8,128)S(1)}, u32[]{:S(2)}, u32[]{:S(2)}) collective-permute-start(f32[392,128]{1,0:T(8,128)S(1)} %get-tuple-element.29), channel_id=1, source_target_pairs={{0,5},{4,9},{8,13},{12,0},{1,4},{5,8},{9,12},{13,1},{2,7},{6,11},{... | collective-permute-start | bytes 602120 | tf_op jit(solution)/shard_map/ppermute | solution.py:258
  16.6 25.2 %collective-permute-start.5 = (f32[392,128]{1,0:T(8,128)S(1)}, f32[392,128]{1,0:T(8,128)S(1)}, u32[]{:S(2)}, u32[]{:S(2)}) collective-permute-start(f32[392,128]{1,0:T(8,128)S(1)} %get-tuple-element.30), channel_id=1, source_target_pairs={{0,9},{4,13},{8,0},{12,4},{1,8},{5,12},{9,1},{13,5},{2,11},{6,15},... | collective-permute-start | bytes 602120 | tf_op jit(solution)/shard_map/ppermute | solution.py:258
  26.5 15.3 %collective-permute-start.6 = (f32[392,128]{1,0:T(8,128)S(1)}, f32[392,128]{1,0:T(8,128)S(1)}, u32[]{:S(2)}, u32[]{:S(2)}) collective-permute-start(f32[392,128]{1,0:T(8,128)S(1)} %get-tuple-element.31), channel_id=1, source_target_pairs={{0,13},{4,0},{8,4},{12,8},{1,12},{5,1},{9,5},{13,9},{2,15},{6,2},{... | collective-permute-start | bytes 602120 | tf_op jit(solution)/shard_map/ppermute | solution.py:258
  44.1 5.6 %collective-permute-start.7 = (f32[128,256]{1,0:T(8,128)S(1)}, f32[128,256]{1,0:T(8,128)S(1)}, u32[]{:S(2)}, u32[]{:S(2)}) collective-permute-start(f32[128,256]{1,0:T(8,128)S(1)} %shard_map.83), channel_id=1, source_target_pairs={{0,2},{4,6},{8,10},{12,14},{1,3},{5,7},{9,11},{13,15},{16,18},{20,... | collective-permute-start | bytes 393224 | tf_op jit(solution)/shard_map/ppermute | solution.py:321
  47.8 29.6 %copy-start.1 = (bf16[256,1024]{1,0:T(8,128)(2,1)S(1)}, bf16[256,1024]{1,0:T(8,128)(2,1)}, u32[]{:S(2)}) copy-start(bf16[256,1024]{1,0:T(8,128)(2,1)} %k_ref.1) | copy-start | bytes 1572868
  47.8 29.6 %copy-start.3 = (bf16[256,1024]{1,0:T(8,128)(2,1)S(1)}, bf16[256,1024]{1,0:T(8,128)(2,1)}, u32[]{:S(2)}) copy-start(bf16[256,1024]{1,0:T(8,128)(2,1)} %v_ref.1) | copy-start | bytes 1572868
  47.8 29.6 %copy-start.4 = (bf16[256,1024]{1,0:T(8,128)(2,1)S(1)}, bf16[256,1024]{1,0:T(8,128)(2,1)}, u32[]{:S(2)}) copy-start(bf16[256,1024]{1,0:T(8,128)(2,1)} %q_ref.1) | copy-start | bytes 1572868
  51.8 10.6 %collective-permute-start.8 = (f32[128,256]{1,0:T(8,128)S(1)}, f32[128,256]{1,0:T(8,128)S(1)}, u32[]{:S(2)}, u32[]{:S(2)}) collective-permute-start(f32[128,256]{1,0:T(8,128)S(1)} %get-tuple-element.33), channel_id=1, source_target_pairs={{0,4},{4,8},{8,12},{12,1},{1,5},{5,9},{9,13},{13,0},{2,6},{6,10},{... | collective-permute-start | bytes 393224 | tf_op jit(solution)/shard_map/ppermute | solution.py:258
  57.0 11.1 %collective-permute-start.9 = (f32[128,256]{1,0:T(8,128)S(1)}, f32[128,256]{1,0:T(8,128)S(1)}, u32[]{:S(2)}, u32[]{:S(2)}) collective-permute-start(f32[128,256]{1,0:T(8,128)S(1)} %get-tuple-element.34), channel_id=1, source_target_pairs={{0,8},{4,12},{8,1},{12,5},{1,9},{5,13},{9,0},{13,4},{2,10},{6,14},... | collective-permute-start | bytes 393224 | tf_op jit(solution)/shard_map/ppermute | solution.py:258
  58.4 22.9 %collective-permute-start.10 = (f32[128,256]{1,0:T(8,128)S(1)}, f32[128,256]{1,0:T(8,128)S(1)}, u32[]{:S(2)}, u32[]{:S(2)}) collective-permute-start(f32[128,256]{1,0:T(8,128)S(1)} %get-tuple-element.35), channel_id=1, source_target_pairs={{0,12},{4,1},{8,5},{12,9},{1,13},{5,0},{9,4},{13,8},{2,14},{6,3},{... | collective-permute-start | bytes 393224 | tf_op jit(solution)/shard_map/ppermute | solution.py:258
  60.3 21.0 %collective-permute-start.11 = (f32[128,256]{1,0:T(8,128)S(1)}, f32[128,256]{1,0:T(8,128)S(1)}, u32[]{:S(2)}, u32[]{:S(2)}) collective-permute-start(f32[128,256]{1,0:T(8,128)S(1)} %get-tuple-element.36), channel_id=1, source_target_pairs={{0,1},{4,5},{8,9},{12,13},{1,0},{5,4},{9,8},{13,12},{2,3},{6,7},{1... | collective-permute-start | bytes 393224 | tf_op jit(solution)/shard_map/ppermute | solution.py:258
  60.3 21.0 %collective-permute-start.12 = (f32[128,256]{1,0:T(8,128)S(1)}, f32[128,256]{1,0:T(8,128)S(1)}, u32[]{:S(2)}, u32[]{:S(2)}) collective-permute-start(f32[128,256]{1,0:T(8,128)S(1)} %get-tuple-element.37), channel_id=1, source_target_pairs={{0,5},{4,9},{8,13},{12,0},{1,4},{5,8},{9,12},{13,1},{2,7},{6,11},{... | collective-permute-start | bytes 393224 | tf_op jit(solution)/shard_map/ppermute | solution.py:258
  62.5 18.9 %collective-permute-start.13 = (f32[128,256]{1,0:T(8,128)S(1)}, f32[128,256]{1,0:T(8,128)S(1)}, u32[]{:S(2)}, u32[]{:S(2)}) collective-permute-start(f32[128,256]{1,0:T(8,128)S(1)} %get-tuple-element.38), channel_id=1, source_target_pairs={{0,9},{4,13},{8,0},{12,4},{1,8},{5,12},{9,1},{13,5},{2,11},{6,15},... | collective-permute-start | bytes 393224 | tf_op jit(solution)/shard_map/ppermute | solution.py:258
  68.1 13.3 %collective-permute-start.14 = (f32[128,256]{1,0:T(8,128)S(1)}, f32[128,256]{1,0:T(8,128)S(1)}, u32[]{:S(2)}, u32[]{:S(2)}) collective-permute-start(f32[128,256]{1,0:T(8,128)S(1)} %get-tuple-element.39), channel_id=1, source_target_pairs={{0,13},{4,0},{8,4},{12,8},{1,12},{5,1},{9,5},{13,9},{2,15},{6,2},{... | collective-permute-start | bytes 393224 | tf_op jit(solution)/shard_map/ppermute | solution.py:258

commit v3 on v2

v3 whole, which is shorter than its diff:
```python
import functools

import jax
import jax.numpy as jnp
from jax import lax
from jax.experimental import pallas as pl
from jax.experimental.pallas import tpu as pltpu
from jax.sharding import PartitionSpec as P

FIRSTS = (1, 2, 3, 4, 5, 6, 7)
ORDER = (2, 4, 6, 3, 5, 1, 7)
READ = 1
HELD = 6
EARLY = 5
TAIL = 8
EPS = 1e-06
EXACT = lax.Precision.HIGHEST


def halves(x):
    high = x.astype(jnp.bfloat16)
    return high, (x - high.astype(jnp.float32)).astype(jnp.bfloat16)


def mul(a, b, dims):
    return lax.dot_general(a, b, (dims, ((), ())), preferred_element_type=jnp.float32)


def mul_tn(a, b):
    return mul(a, b, ((0,), (0,)))


def mul_nt(a, b):
    return mul(a, b, ((1,), (1,)))


def mul_nn(a, b):
    return mul(a, b, ((1,), (0,)))


def exact(a, b):
    return jnp.dot(a, b, precision=EXACT, preferred_element_type=jnp.float32)


def grid_ids(shape):
    return lax.broadcasted_iota(jnp.int32, shape, 0), lax.broadcasted_iota(jnp.int32, shape, 1)


def lanes_of(h, width):
    return pl.ds(pl.multiple_of(h * width, width), width)


def map_kernel(heads, width, shifts, mine_ref, *refs):
    hbm, outs = refs[:5], refs[5 : 5 + len(shifts)]
    *held, sem = refs[5 + len(shifts) :]
    k_ref, v_ref, retain_ref, step_ref, momentum_ref = held
    copies = [pltpu.make_async_copy(s, t, sem.at[n]) for n, (s, t) in enumerate(zip(hbm, held))]
    for copy in copies[2:] + copies[:2]:
        copy.start()
    mine = mine_ref[0]
    length = k_ref.shape[0]
    row, col = grid_ids((length, length))
    before = (row <= col).astype(jnp.float32)
    after = (row >= col).astype(jnp.float32)
    drow, dcol = grid_ids((width, width))
    keep = drow <= dcol
    diagonal = drow == dcol
    for copy in copies[2:]:
        copy.wait()
    from_mine = lambda ref: pltpu.roll(ref[...], lax.rem(heads - mine, heads), 0)
    step = from_mine(step_ref)
    logs = exact(
        jnp.concatenate([jnp.log(from_mine(retain_ref)), jnp.log(from_mine(momentum_ref))], axis=0), before
    )
    log_retain, log_moment = logs[:heads], logs[heads:]
    decay = jnp.exp(log_moment)
    reach = jnp.exp(log_retain[:, length - 1 :] - log_retain) * decay
    suffix = exact(reach, after)
    memory_weight = (suffix / decay * step).T
    moment_weight = (jnp.exp(log_moment[:, length - 1 :] - log_moment) * step).T
    retain_end = jnp.exp(log_retain[:, length - 1 :])
    moment_end = decay[:, length - 1 :]
    carry_end = suffix[:, :1]
    for copy in copies[:2]:
        copy.wait()
    for n, s in enumerate(shifts):
        lanes = lanes_of(lax.rem(mine + s, heads), width)
        keys = k_ref[:, lanes]
        values = v_ref[:, lanes]
        wide = keys.astype(jnp.float32)
        scale = lax.rsqrt(jnp.sum(wide * wide, -1, keepdims=True) + EPS)
        weight_m = memory_weight[:, s : s + 1] * scale
        weight_s = moment_weight[:, s : s + 1] * scale
        write = jnp.concatenate([wide * weight_m, wide * weight_s], axis=1)
        high, low = halves(write)
        offset = mul_tn(values, high) + mul_tn(values, low)
        high, low = halves(write * scale)
        gram = mul_tn(keys, high) + mul_tn(keys, low)
        moment_gram = gram[:, width:]
        on_diagonal = jnp.sum(jnp.where(diagonal, moment_gram, 0.0), axis=0, keepdims=True)
        wide_row = lambda x: jnp.broadcast_to(x[s : s + 1, :], (1, width))
        out = outs[n]
        out[:width, :] = jnp.where(keep, gram[:, :width], moment_gram)
        out[width : 2 * width, :] = offset[:, :width]
        out[2 * width : 3 * width, :] = offset[:, width:]
        out[3 * width :, :] = jnp.concatenate(
            [
                on_diagonal,
                wide_row(retain_end),
                wide_row(moment_end),
                wide_row(carry_end),
                jnp.zeros((TAIL - 4, width), jnp.float32),
            ],
            axis=0,
        )


def read_kernel(
    heads, width, q_ref, k_ref, v_ref, retain_ref, step_ref, momentum_ref, high_ref, low_ref, base_ref
):
    length = k_ref.shape[0]
    row, col = grid_ids((length, length))
    before = (row <= col).astype(jnp.float32)
    causal = row >= col
    lower = causal.astype(jnp.bfloat16)
    logs = exact(jnp.concatenate([jnp.log(retain_ref[...]), jnp.log(momentum_ref[...])], axis=0), before)
    log_retain, log_moment = logs[:heads], logs[heads:]
    log_gap = log_moment - log_retain
    step_rows = step_ref[...] * jnp.exp(-log_moment)
    log_column = log_retain.T
    retain_scale = jnp.exp(log_column)
    ones = jnp.ones((8, width), jnp.bfloat16)
    for h in range(heads):
        lanes = slice(h * width, (h + 1) * width)
        queries, keys, values = q_ref[:, lanes], k_ref[:, lanes], v_ref[:, lanes]
        wide_q = queries.astype(jnp.float32)
        wide_k = keys.astype(jnp.float32)
        query_scale = lax.rsqrt(jnp.sum(wide_q * wide_q, -1, keepdims=True) + EPS)
        high, low = halves(wide_k * wide_k)
        key_scale = lax.rsqrt((mul_nt(ones, high) + mul_nt(ones, low))[:1, :] + EPS)
        gap = log_column[:, h : h + 1] + log_gap[h : h + 1, :]
        reach = jnp.exp(jnp.where(causal, gap, -1e30))
        high, low = halves(reach)
        weights = mul_nn(high, lower) + mul_nn(low, lower)
        mixing = mul_nt(queries, keys) * weights * (step_rows[h : h + 1, :] * key_scale)
        high, low = halves(mixing)
        base_ref[h] = query_scale * (mul_nn(high, values) + mul_nn(low, values))
        high, low = halves(mixing * key_scale)
        seen = mul_nn(high, keys) + mul_nn(low, keys)
        unit_q = query_scale * wide_q
        reads = jnp.concatenate(
            [retain_scale[:, h : h + 1] * unit_q - query_scale * seen, weights[:, :1] * unit_q], axis=1
        )
        high, low = halves(reads)
        high_ref[h] = high
        low_ref[h] = low


def steps(width, state, high_ref, low_ref, offset_ref, count, keep=None):
    for b in range(count):
        if keep is not None:
            keep[b] = state
        tail = offset_ref[b, 2 * width :, :]
        memory, moment = state[:, :width], state[:, width:]
        high, low = halves(memory)
        seen = mul_nn(high, high_ref[b]) + (mul_nn(high, low_ref[b]) + mul_nn(low, high_ref[b]))
        new_memory = tail[1:2, :] * memory + tail[3:4, :] * moment + offset_ref[b, :width, :] - seen[:, :width]
        new_moment = tail[2:3, :] * moment + offset_ref[b, width : 2 * width, :] - seen[:, width:]
        state = jnp.concatenate([new_memory, new_moment], axis=1)
    return state


def unpack_kernel(heads, width, order, mine_ref, entry_ref, *refs):
    arrived, (high_ref, low_ref, offset_ref, final_ref) = refs[:heads], refs[heads:]
    mine = mine_ref[0]
    row, col = grid_ids((width, width))
    for n, s in enumerate(order):
        b = lax.rem(mine + heads - s, heads)
        packed = arrived[n][:width, :]
        flipped = packed.T
        diagonal = arrived[n][3 * width : 3 * width + 1, :]
        gram = jnp.concatenate(
            [
                jnp.where(row <= col, packed, flipped),
                jnp.where(row == col, diagonal, jnp.where(row > col, packed, flipped)),
            ],
            axis=1,
        )
        high, low = halves(gram)
        high_ref[b] = high
        low_ref[b] = low
        offset_ref[b] = arrived[n][width:, :]
    final_ref[...] = steps(width, entry_ref[...], high_ref, low_ref, offset_ref, heads)


def final_kernel(heads, width, flag_ref, entry_ref, other_ref, high_ref, low_ref, offset_ref, kept_ref, final_ref):
    entry = jnp.where(flag_ref[0] > 0, other_ref[...], entry_ref[...])
    kept_ref[...] = entry
    final_ref[...] = steps(width, entry, high_ref, low_ref, offset_ref, heads)


def states_kernel(heads, width, scalar_ref, entry_ref, other_ref, high_ref, low_ref, offset_ref, *refs):
    outs, keep = refs[:heads], refs[heads]
    mine = scalar_ref[1]
    entry = jnp.where(scalar_ref[0] > 0, other_ref[...], entry_ref[...])
    keep[heads - 1] = steps(width, entry, high_ref, low_ref, offset_ref, heads - 1, keep)
    for s in range(heads):
        outs[s][...] = keep[lax.rem(mine + s, heads)]


def read_out(h, state, read_high_ref, read_low_ref, base_ref):
    high, low = halves(state)
    read_high = read_high_ref[h]
    result = base_ref[h] + mul_nt(read_high, high)
    return (result + (mul_nt(read_high, low) + mul_nt(read_low_ref[h], high))).astype(jnp.bfloat16)


def early_kernel(heads, mine_ref, read_high_ref, read_low_ref, base_ref, *refs):
    *arrived, out_ref = refs
    mine = mine_ref[0]
    for s, ref in enumerate(arrived):
        h = lax.rem(mine + heads - s, heads)
        out_ref[s] = read_out(h, ref[...], read_high_ref, read_low_ref, base_ref)


def output_kernel(heads, width, mine_ref, read_high_ref, read_low_ref, base_ref, early_ref, *refs):
    *arrived, out_ref = refs
    mine = mine_ref[0]
    early = heads - len(arrived)
    for s in range(heads):
        h = lax.rem(mine + heads - s, heads)
        if s < early:
            result = early_ref[s]
        else:
            result = read_out(h, arrived[s - early][...], read_high_ref, read_low_ref, base_ref)
        out_ref[:, lanes_of(h, width)] = result


VMEM = pl.BlockSpec(memory_space=pltpu.VMEM)
HBM = pl.BlockSpec(memory_space=pltpu.HBM)
SMEM = pl.BlockSpec(memory_space=pltpu.SMEM)
LIMIT = pltpu.CompilerParams(vmem_limit_bytes=24 << 20)


def shape(kind, *sizes):
    return jax.ShapeDtypeStruct(sizes, kind)


def local(n_outer, n_inner, queries, keys, values, retain, step, momentum, init_memory, init_moment):
    length, heads = retain.shape
    width = init_memory.shape[2]
    f32, bf16 = jnp.float32, jnp.bfloat16
    axes = ("inner", "outer")
    place = lambda f: (f % n_inner) * n_outer + f // n_inner
    sections = n_outer * n_inner // heads
    teams = [[place(s * heads + j) for j in range(heads)] for s in range(sections)]
    position = lax.axis_index("outer") * n_inner + lax.axis_index("inner")
    section, mine = position // heads, position % heads
    scalars = lambda *xs: jnp.stack([jnp.asarray(x).astype(jnp.int32) for x in xs])
    gates = (retain.T, step.T, momentum.T)

    def call(kernel, out, given, spaces=VMEM, scratch=(), outs=VMEM):
        return pl.pallas_call(
            kernel,
            out_shape=out,
            in_specs=[SMEM] + [spaces] * (len(given) - 1),
            out_specs=jax.tree.map(lambda _: outs, out),
            scratch_shapes=scratch,
            compiler_params=LIMIT,
        )(*given)

    def shift(piece, s):
        pairs = [(team[j], team[(j + s) % heads]) for team in teams for j in range(heads)]
        return lax.ppermute(piece, axes, pairs)

    turns = [s for s in ORDER if s < heads]

    def swap(pieces):
        moved = {0: pieces[0], **{s: shift(pieces[s], s) for s in turns}}
        return [moved[s] for s in range(heads)]

    def behind(xs, y):
        return list(lax.optimization_barrier((*xs, y))[:-1])

    def make(shifts, given):
        given = [pltpu.with_memory_space_constraint(x, pltpu.HBM) for x in given]
        return call(
            functools.partial(map_kernel, heads, width, shifts),
            [shape(f32, 3 * width + TAIL, width)] * len(shifts),
            (scalars(mine), *given),
            HBM,
            [pltpu.VMEM(x.shape, x.dtype) for x in given] + [pltpu.SemaphoreType.DMA((len(given),))],
        )

    order = [*FIRSTS, 0]
    made = dict(zip(order, make(order, (keys, values, *gates))))
    maps = {0: made[0], **{s: shift(made[s], s) for s in order[:-1]}}
    maps = [maps[s] for s in order]

    start = jnp.concatenate(
        [
            lax.dynamic_index_in_dim(init_memory, mine, 0, keepdims=False),
            lax.dynamic_index_in_dim(init_moment, mine, 0, keepdims=False),
        ],
        axis=1,
    )
    state = shape(f32, width, 2 * width)
    *unpacked, final = call(
        functools.partial(unpack_kernel, heads, width, order),
        [
            shape(bf16, heads, width, 2 * width),
            shape(bf16, heads, width, 2 * width),
            shape(f32, heads, 2 * width + TAIL, width),
            state,
        ],
        (scalars(mine), start, *maps),
    )
    entry, other, flag = start, start, section < 0
    for s in range(sections - 1):
        if s > 0:
            entry, final = call(
                functools.partial(final_kernel, heads, width), [state] * 2, (scalars(flag), entry, other, *unpacked)
            )
        other = lax.ppermute(final, axes, list(zip(teams[s], teams[s + 1])))
        flag = section == s + 1
    states = call(
        functools.partial(states_kernel, heads, width),
        [state] * heads,
        (scalars(flag, mine), entry, other, *unpacked),
        scratch=[pltpu.VMEM((heads, width, 2 * width), f32)],
    )
    pieces, moved = states, {0: states[0]}
    for n, s in enumerate(turns):
        if n == READ:
            given = behind((queries, keys, values, *gates), moved[turns[0]])
            reads = pl.pallas_call(
                functools.partial(read_kernel, heads, width),
                out_shape=[
                    shape(bf16, heads, length, 2 * width),
                    shape(bf16, heads, length, 2 * width),
                    shape(f32, heads, length, width),
                ],
                in_specs=[VMEM] * 6,
                out_specs=[VMEM] * 3,
                compiler_params=LIMIT,
            )(*given,)
        piece = pieces[s] if n < HELD else behind([pieces[s]], reads[2])[0]
        moved[s] = shift(piece, s)
    states = [moved[s] for s in range(heads)]
    early = call(
        functools.partial(early_kernel, heads),
        shape(bf16, EARLY, length, width),
        (scalars(mine), *reads, *states[:EARLY]),
    )
    return call(
        functools.partial(output_kernel, heads, width),
        shape(bf16, length, heads * width),
        (scalars(mine), *reads, early, *states[EARLY:]),
    )


def solution(mesh):
    rows = P(("groups", "outer", "inner"), None)
    return jax.shard_map(
        functools.partial(local, mesh.shape["outer"], mesh.shape["inner"]),
        mesh=mesh,
        in_specs=(rows,) * 6 + (P(), P()),
        out_specs=rows,
        check_vma=False,
    )
```

time: 83.7 us -> 79.1 us (0.945)
  the two profiles are of different devices: /device:TPU:1 before, /device:TPU:11 now
where the time goes in v3:
time: 79.1 us; the launch traced here: 78.9 us
  waiting for transfers between devices  41.7 us (53%)
  starting transfers between devices  22 us (28%)
  Pallas kernels  14.1 us (18%)
  local copies, waits for them, and re-layouts  0.91 us (1%)
    ppermute x14, waiting for transfers between devices, shift(): return lax.ppermute(piece, axes, pairs)  36.3 us
    ppermute x14, starting transfers between devices, shift(): return lax.ppermute(piece, axes, pairs)  20.7 us
    pallas_call x5, Pallas kernels, call(): pl.pallas_call(kernel, out_shape=out, in_specs=[SMEM] + [spaces] * (len(g...  10.4 us
    ppermute x1, waiting for transfers between devices, local(): other = lax.ppermute(final, axes, list(zip(teams[s], teams[s + 1])))  5.37 us
    pallas_call x1, Pallas kernels, local(): pl.pallas_call(functools.partial(read_kernel, heads, width), out_shape=[s...  3.77 us
  transfers between devices with their start and end apart: 15, of which 10 were waited for; matrix products, arithmetic and copies ran while one was open for 1% of the time, Pallas kernels for 6%

profile of v3, /device:TPU:11, one launch (start us, length us, event | category | flops | bytes accessed | tf_op | source)
XLA Modules:
  0.0 78.9 jit_solution(14887439334852196433)
XLA Ops:
  0.0 3.9 %shard_map.82 = (f32[392,128]{1,0:T(8,128)S(1)}, f32[392,128]{1,0:T(8,128)S(1)}, f32[392,128]{1,0:T(8,128)S(1)}, f32[392,128]{1,0:T(8,128)S(1)}, f32[392,128]{1,...) custom-call(s32[1]{0:T(128)} %bitcast.mine_ref, bf16[256,1024]{1,0:T(8,128)(2,1)} %k_ref, ...), custom_call_target="tpu_custom_call" | custom-call | tf_op jit(solution)/shard_map/pallas_call | solution.py:263
  3.9 1.4 %collective-permute-start = (f32[392,128]{1,0:T(8,128)S(1)}, f32[392,128]{1,0:T(8,128)S(1)}, u32[]{:S(2)}, u32[]{:S(2)}) collective-permute-start(f32[392,128]{1,0:T(8,128)S(1)} %get-tuple-element.35), channel_id=1, source_target_pairs={{0,4},{4,8},{8,12},{12,1},{1,5},{5,9},{9,13},{13,0},{2,6},{6,10},{... | collective-permute-start | bytes 602120 | tf_op jit(solution)/shard_map/ppermute | solution.py:274
  5.2 1.5 %collective-permute-start.1 = (f32[392,128]{1,0:T(8,128)S(1)}, f32[392,128]{1,0:T(8,128)S(1)}, u32[]{:S(2)}, u32[]{:S(2)}) collective-permute-start(f32[392,128]{1,0:T(8,128)S(1)} %get-tuple-element.36), channel_id=1, source_target_pairs={{0,8},{4,12},{8,1},{12,5},{1,9},{5,13},{9,0},{13,4},{2,10},{6,14},... | collective-permute-start | bytes 602120 | tf_op jit(solution)/shard_map/ppermute | solution.py:274
  6.8 2.1 %collective-permute-start.2 = (f32[392,128]{1,0:T(8,128)S(1)}, f32[392,128]{1,0:T(8,128)S(1)}, u32[]{:S(2)}, u32[]{:S(2)}) collective-permute-start(f32[392,128]{1,0:T(8,128)S(1)} %get-tuple-element.37), channel_id=1, source_target_pairs={{0,12},{4,1},{8,5},{12,9},{1,13},{5,0},{9,4},{13,8},{2,14},{6,3},{... | collective-permute-start | bytes 602120 | tf_op jit(solution)/shard_map/ppermute | solution.py:274
  9.8 5.4 %collective-permute-start.5 = (f32[392,128]{1,0:T(8,128)S(1)}, f32[392,128]{1,0:T(8,128)S(1)}, u32[]{:S(2)}, u32[]{:S(2)}) collective-permute-start(f32[392,128]{1,0:T(8,128)S(1)} %get-tuple-element.40), channel_id=1, source_target_pairs={{0,9},{4,13},{8,0},{12,4},{1,8},{5,12},{9,1},{13,5},{2,11},{6,15},... | collective-permute-start | bytes 602120 | tf_op jit(solution)/shard_map/ppermute | solution.py:274
  15.2 6.6 %collective-permute-done.1.refs_1_ = f32[392,128]{1,0:T(8,128)S(1)} collective-permute-done((f32[392,128]{1,0:T(8,128)S(1)}, f32[392,128]{1,0:T(8,128)S(1)}, u32[]{:S(2)}, u32[]{:S(2)}) %collective-permute-start.1) | collective-permute-done | bytes 200736 | tf_op jit(solution)/shard_map/ppermute | solution.py:274
  21.8 1.7 %collective-permute-start.6 = (f32[392,128]{1,0:T(8,128)S(1)}, f32[392,128]{1,0:T(8,128)S(1)}, u32[]{:S(2)}, u32[]{:S(2)}) collective-permute-start(f32[392,128]{1,0:T(8,128)S(1)} %get-tuple-element.41), channel_id=1, source_target_pairs={{0,13},{4,0},{8,4},{12,8},{1,12},{5,1},{9,5},{13,9},{2,15},{6,2},{... | collective-permute-start | bytes 602120 | tf_op jit(solution)/shard_map/ppermute | solution.py:274
  23.5 0.9 %dynamic-slice_bitcast_fusion = (f32[128,128]{1,0:T(8,128)S(1)}, f32[128,128]{1,0:T(8,128)S(1)}) fusion(f32[8,128,128]{2,1,0:T(8,128)} %param.15, s32[]{:T(128)S(6)} %select_n.18, f32[8,128,128]{2,1,0:T(8,128)} %param.14), kind=kLoop, calls=%fused_computation.1 | loop fusion | bytes 262148 | tf_op jit(solution)/shard_map/jit(dynamic_index_in_dim)/squeeze | solution.py:303
  24.4 9.4 %collective-permute-done.2.refs_2_ = f32[392,128]{1,0:T(8,128)S(1)} collective-permute-done((f32[392,128]{1,0:T(8,128)S(1)}, f32[392,128]{1,0:T(8,128)S(1)}, u32[]{:S(2)}, u32[]{:S(2)}) %collective-permute-start.2) | collective-permute-done | bytes 200736 | tf_op jit(solution)/shard_map/ppermute | solution.py:274
  33.8 5.2 %collective-permute-done.5.refs_5_ = f32[392,128]{1,0:T(8,128)S(1)} collective-permute-done((f32[392,128]{1,0:T(8,128)S(1)}, f32[392,128]{1,0:T(8,128)S(1)}, u32[]{:S(2)}, u32[]{:S(2)}) %collective-permute-start.5) | collective-permute-done | bytes 200736 | tf_op jit(solution)/shard_map/ppermute | solution.py:274
  39.0 3.4 %collective-permute-done.6.refs_6_ = f32[392,128]{1,0:T(8,128)S(1)} collective-permute-done((f32[392,128]{1,0:T(8,128)S(1)}, f32[392,128]{1,0:T(8,128)S(1)}, u32[]{:S(2)}, u32[]{:S(2)}) %collective-permute-start.6) | collective-permute-done | bytes 200736 | tf_op jit(solution)/shard_map/ppermute | solution.py:274
  42.5 2.5 %shard_map.83 = (bf16[8,128,256]{2,1,0:T(8,128)(2,1)S(1)}, bf16[8,128,256]{2,1,0:T(8,128)(2,1)S(1)}, f32[8,264,128]{2,1,0:T(8,128)S(1)}, f32[128,256]{1,0:T(8,128)}) custom-call(s32[1]{0:T(128)} %bitcast.mine_ref, f32[128,256]{1,0:T(8,128)S(1)} %pad_maximum_fusion.entry_ref, f32[392,128]{1,0:T(8,128)S(1)} %collective-permute-done.refs_0_, ...), custom_call_target="tpu_custom_call" | custom-call | tf_op jit(solution)/shard_map/pallas_call | solution.py:263
  45.0 1.3 %collective-permute-start.7 = (f32[128,256]{1,0:T(8,128)}, f32[128,256]{1,0:T(8,128)S(1)}, u32[]{:S(2)}, u32[]{:S(2)}) collective-permute-start(f32[128,256]{1,0:T(8,128)} %get-tuple-element.43), channel_id=1, source_target_pairs={{0,2},{4,6},{8,10},{12,14},{1,3},{5,7},{9,11},{13,15},{16,18},{20,... | collective-permute-start | bytes 393224 | tf_op jit(solution)/shard_map/ppermute | solution.py:324
  46.4 5.4 %collective-permute-done.7.other_ref = f32[128,256]{1,0:T(8,128)S(1)} collective-permute-done((f32[128,256]{1,0:T(8,128)}, f32[128,256]{1,0:T(8,128)S(1)}, u32[]{:S(2)}, u32[]{:S(2)}) %collective-permute-start.7) | collective-permute-done | bytes 131104 | tf_op jit(solution)/shard_map/ppermute | solution.py:324
  51.8 2.0 %shard_map.84 = (f32[128,256]{1,0:T(8,128)S(1)}, f32[128,256]{1,0:T(8,128)S(1)}, f32[128,256]{1,0:T(8,128)S(1)}, f32[128,256]{1,0:T(8,128)S(1)}, f32[128,256]{1,...) custom-call(s32[2]{0:T(128)S(1)} %pad_add_fusion.scalar_ref, ...), custom_call_target="tpu_custom_call" | custom-call | tf_op jit(solution)/shard_map/pallas_call | solution.py:263
  53.7 1.4 %collective-permute-start.8 = (f32[128,256]{1,0:T(8,128)S(1)}, f32[128,256]{1,0:T(8,128)S(1)}, u32[]{:S(2)}, u32[]{:S(2)}) collective-permute-start(f32[128,256]{1,0:T(8,128)S(1)} %get-tuple-element.47), channel_id=1, source_target_pairs={{0,8},{4,12},{8,1},{12,5},{1,9},{5,13},{9,0},{13,4},{2,10},{6,14},... | collective-permute-start | bytes 393224 | tf_op jit(solution)/shard_map/ppermute | solution.py:274
  55.2 2.3 %collective-permute-start.10 = (f32[128,256]{1,0:T(8,128)S(1)}, f32[128,256]{1,0:T(8,128)S(1)}, u32[]{:S(2)}, u32[]{:S(2)}) collective-permute-start(f32[128,256]{1,0:T(8,128)S(1)} %get-tuple-element.59), channel_id=1, source_target_pairs={{0,12},{4,1},{8,5},{12,9},{1,13},{5,0},{9,4},{13,8},{2,14},{6,3},{... | collective-permute-start | bytes 393224 | tf_op jit(solution)/shard_map/ppermute | solution.py:274
  58.0 2.3 %collective-permute-done.8.refs_2_ = f32[128,256]{1,0:T(8,128)S(1)} collective-permute-done((f32[128,256]{1,0:T(8,128)S(1)}, f32[128,256]{1,0:T(8,128)S(1)}, u32[]{:S(2)}, u32[]{:S(2)}) %collective-permute-start.8) | collective-permute-done | bytes 131104 | tf_op jit(solution)/shard_map/ppermute | solution.py:274
  60.3 4.2 %collective-permute-start.13 = (f32[128,256]{1,0:T(8,128)S(1)}, f32[128,256]{1,0:T(8,128)S(1)}, u32[]{:S(2)}, u32[]{:S(2)}) collective-permute-start(f32[128,256]{1,0:T(8,128)S(1)} %get-tuple-element.62), channel_id=1, source_target_pairs={{0,9},{4,13},{8,0},{12,4},{1,8},{5,12},{9,1},{13,5},{2,11},{6,15},... | collective-permute-start | bytes 393224 | tf_op jit(solution)/shard_map/ppermute | solution.py:274
  64.5 3.8 %shard_map.85 = (bf16[8,256,256]{2,1,0:T(8,128)(2,1)S(1)}, bf16[8,256,256]{2,1,0:T(8,128)(2,1)S(1)}, f32[8,256,128]{2,1,0:T(8,128)S(1)}) custom-call(bf16[256,1024]{1,0:T(8,128)(2,1)S(1)} %copy-done.2, bf16[256,1024]{1,0:T(8,128)(2,1)S(1)} %copy-done, bf16[256,1024]{1,0:T(8,128)(2,1)S(1)} %copy-done.1, f32[8,256]{1,0:T(8,128)S(1)} %bitcast.10, ...), custom_call_target="tpu_custom_call" | custom-call | tf_op jit(solution)/shard_map/pallas_call | solution.py:336
  69.1 4.6 %collective-permute-done.12.refs_0_ = f32[128,256]{1,0:T(8,128)S(1)} collective-permute-done((f32[128,256]{1,0:T(8,128)S(1)}, f32[128,256]{1,0:T(8,128)S(1)}, u32[]{:S(2)}, u32[]{:S(2)}) %collective-permute-start.12) | collective-permute-done | bytes 131104 | tf_op jit(solution)/shard_map/ppermute | solution.py:274
  73.8 2.8 %collective-permute-done.13.refs_1_ = f32[128,256]{1,0:T(8,128)S(1)} collective-permute-done((f32[128,256]{1,0:T(8,128)S(1)}, f32[128,256]{1,0:T(8,128)S(1)}, u32[]{:S(2)}, u32[]{:S(2)}) %collective-permute-start.13) | collective-permute-done | bytes 131104 | tf_op jit(solution)/shard_map/ppermute | solution.py:274
  76.6 1.0 %collective-permute-done.14.refs_2_ = f32[128,256]{1,0:T(8,128)S(1)} collective-permute-done((f32[128,256]{1,0:T(8,128)S(1)}, f32[128,256]{1,0:T(8,128)S(1)}, u32[]{:S(2)}, u32[]{:S(2)}) %collective-permute-start.14) | collective-permute-done | bytes 131104 | tf_op jit(solution)/shard_map/ppermute | solution.py:274
  77.6 1.3 %shard_map.87 = bf16[256,1024]{1,0:T(8,128)(2,1)} custom-call(s32[1]{0:T(128)} %bitcast.mine_ref, bf16[8,256,256]{2,1,0:T(8,128)(2,1)S(1)} %get-tuple-element.54.read_high_ref, bf16[8,256,256]{2,1,0:T(8,128)(2,1)S(1)} %get-tuple-element.55.read_low_ref, f32[8,256,128]{2,1,0:T(8,128)S(1)} %get-tuple-element.56.base_ref, ...), custom_call_target="tpu_custom_call" | custom-call | tf_op jit(solution)/shard_map/pallas_call | solution.py:263
  (27 shorter events, 2.4 us)
Async XLA Ops:
  3.9 5.9 %collective-permute-start = (f32[392,128]{1,0:T(8,128)S(1)}, f32[392,128]{1,0:T(8,128)S(1)}, u32[]{:S(2)}, u32[]{:S(2)}) collective-permute-start(f32[392,128]{1,0:T(8,128)S(1)} %get-tuple-element.35), channel_id=1, source_target_pairs={{0,4},{4,8},{8,12},{12,1},{1,5},{5,9},{9,13},{13,0},{2,6},{6,10},{... | collective-permute-start | bytes 602120 | tf_op jit(solution)/shard_map/ppermute | solution.py:274
  5.2 16.6 %collective-permute-start.1 = (f32[392,128]{1,0:T(8,128)S(1)}, f32[392,128]{1,0:T(8,128)S(1)}, u32[]{:S(2)}, u32[]{:S(2)}) collective-permute-start(f32[392,128]{1,0:T(8,128)S(1)} %get-tuple-element.36), channel_id=1, source_target_pairs={{0,8},{4,12},{8,1},{12,5},{1,9},{5,13},{9,0},{13,4},{2,10},{6,14},... | collective-permute-start | bytes 602120 | tf_op jit(solution)/shard_map/ppermute | solution.py:274
  6.8 27.1 %collective-permute-start.2 = (f32[392,128]{1,0:T(8,128)S(1)}, f32[392,128]{1,0:T(8,128)S(1)}, u32[]{:S(2)}, u32[]{:S(2)}) collective-permute-start(f32[392,128]{1,0:T(8,128)S(1)} %get-tuple-element.37), channel_id=1, source_target_pairs={{0,12},{4,1},{8,5},{12,9},{1,13},{5,0},{9,4},{13,8},{2,14},{6,3},{... | collective-permute-start | bytes 602120 | tf_op jit(solution)/shard_map/ppermute | solution.py:274
  8.8 25.0 %collective-permute-start.3 = (f32[392,128]{1,0:T(8,128)S(1)}, f32[392,128]{1,0:T(8,128)S(1)}, u32[]{:S(2)}, u32[]{:S(2)}) collective-permute-start(f32[392,128]{1,0:T(8,128)S(1)} %get-tuple-element.38), channel_id=1, source_target_pairs={{0,1},{4,5},{8,9},{12,13},{1,0},{5,4},{9,8},{13,12},{2,3},{6,7},{1... | collective-permute-start | bytes 602120 | tf_op jit(solution)/shard_map/ppermute | solution.py:274
  8.8 25.0 %collective-permute-start.4 = (f32[392,128]{1,0:T(8,128)S(1)}, f32[392,128]{1,0:T(8,128)S(1)}, u32[]{:S(2)}, u32[]{:S(2)}) collective-permute-start(f32[392,128]{1,0:T(8,128)S(1)} %get-tuple-element.39), channel_id=1, source_target_pairs={{0,5},{4,9},{8,13},{12,0},{1,4},{5,8},{9,12},{13,1},{2,7},{6,11},{... | collective-permute-start | bytes 602120 | tf_op jit(solution)/shard_map/ppermute | solution.py:274
  9.8 29.2 %collective-permute-start.5 = (f32[392,128]{1,0:T(8,128)S(1)}, f32[392,128]{1,0:T(8,128)S(1)}, u32[]{:S(2)}, u32[]{:S(2)}) collective-permute-start(f32[392,128]{1,0:T(8,128)S(1)} %get-tuple-element.40), channel_id=1, source_target_pairs={{0,9},{4,13},{8,0},{12,4},{1,8},{5,12},{9,1},{13,5},{2,11},{6,15},... | collective-permute-start | bytes 602120 | tf_op jit(solution)/shard_map/ppermute | solution.py:274
  21.8 20.6 %collective-permute-start.6 = (f32[392,128]{1,0:T(8,128)S(1)}, f32[392,128]{1,0:T(8,128)S(1)}, u32[]{:S(2)}, u32[]{:S(2)}) collective-permute-start(f32[392,128]{1,0:T(8,128)S(1)} %get-tuple-element.41), channel_id=1, source_target_pairs={{0,13},{4,0},{8,4},{12,8},{1,12},{5,1},{9,5},{13,9},{2,15},{6,2},{... | collective-permute-start | bytes 602120 | tf_op jit(solution)/shard_map/ppermute | solution.py:274
  45.0 6.8 %collective-permute-start.7 = (f32[128,256]{1,0:T(8,128)}, f32[128,256]{1,0:T(8,128)S(1)}, u32[]{:S(2)}, u32[]{:S(2)}) collective-permute-start(f32[128,256]{1,0:T(8,128)} %get-tuple-element.43), channel_id=1, source_target_pairs={{0,2},{4,6},{8,10},{12,14},{1,3},{5,7},{9,11},{13,15},{16,18},{20,... | collective-permute-start | bytes 393224 | tf_op jit(solution)/shard_map/ppermute | solution.py:324
  51.7 12.8 %copy-start = (bf16[256,1024]{1,0:T(8,128)(2,1)S(1)}, bf16[256,1024]{1,0:T(8,128)(2,1)}, u32[]{:S(2)}) copy-start(bf16[256,1024]{1,0:T(8,128)(2,1)} %k_ref) | copy-start | bytes 1572868
  51.7 12.8 %copy-start.1 = (bf16[256,1024]{1,0:T(8,128)(2,1)S(1)}, bf16[256,1024]{1,0:T(8,128)(2,1)}, u32[]{:S(2)}) copy-start(bf16[256,1024]{1,0:T(8,128)(2,1)} %v_ref) | copy-start | bytes 1572868
  51.7 12.8 %copy-start.2 = (bf16[256,1024]{1,0:T(8,128)(2,1)S(1)}, bf16[256,1024]{1,0:T(8,128)(2,1)}, u32[]{:S(2)}) copy-start(bf16[256,1024]{1,0:T(8,128)(2,1)} %q_ref) | copy-start | bytes 1572868
  51.8 12.8 %copy-start.3 = (f32[256,8]{0,1:T(8,128)S(1)}, f32[256,8]{0,1:T(8,128)}, u32[]{:S(2)}) copy-start(f32[256,8]{0,1:T(8,128)} %param.11) | copy-start | bytes 24580
  51.8 12.8 %copy-start.4 = (f32[256,8]{0,1:T(8,128)S(1)}, f32[256,8]{0,1:T(8,128)}, u32[]{:S(2)}) copy-start(f32[256,8]{0,1:T(8,128)} %param.12) | copy-start | bytes 24580
  51.8 12.8 %copy-start.5 = (f32[256,8]{0,1:T(8,128)S(1)}, f32[256,8]{0,1:T(8,128)}, u32[]{:S(2)}) copy-start(f32[256,8]{0,1:T(8,128)} %param.13) | copy-start | bytes 24580
  53.7 6.6 %collective-permute-start.8 = (f32[128,256]{1,0:T(8,128)S(1)}, f32[128,256]{1,0:T(8,128)S(1)}, u32[]{:S(2)}, u32[]{:S(2)}) collective-permute-start(f32[128,256]{1,0:T(8,128)S(1)} %get-tuple-element.47), channel_id=1, source_target_pairs={{0,8},{4,12},{8,1},{12,5},{1,9},{5,13},{9,0},{13,4},{2,10},{6,14},... | collective-permute-start | bytes 393224 | tf_op jit(solution)/shard_map/ppermute | solution.py:274
  55.2 13.2 %collective-permute-start.9 = (f32[128,256]{1,0:T(8,128)S(1)}, f32[128,256]{1,0:T(8,128)S(1)}, u32[]{:S(2)}, u32[]{:S(2)}) collective-permute-start(f32[128,256]{1,0:T(8,128)S(1)} %get-tuple-element.58), channel_id=1, source_target_pairs={{0,4},{4,8},{8,12},{12,1},{1,5},{5,9},{9,13},{13,0},{2,6},{6,10},{... | collective-permute-start | bytes 393224 | tf_op jit(solution)/shard_map/ppermute | solution.py:274
  55.2 13.2 %collective-permute-start.10 = (f32[128,256]{1,0:T(8,128)S(1)}, f32[128,256]{1,0:T(8,128)S(1)}, u32[]{:S(2)}, u32[]{:S(2)}) collective-permute-start(f32[128,256]{1,0:T(8,128)S(1)} %get-tuple-element.59), channel_id=1, source_target_pairs={{0,12},{4,1},{8,5},{12,9},{1,13},{5,0},{9,4},{13,8},{2,14},{6,3},{... | collective-permute-start | bytes 393224 | tf_op jit(solution)/shard_map/ppermute | solution.py:274
  57.5 10.9 %collective-permute-start.11 = (f32[128,256]{1,0:T(8,128)S(1)}, f32[128,256]{1,0:T(8,128)S(1)}, u32[]{:S(2)}, u32[]{:S(2)}) collective-permute-start(f32[128,256]{1,0:T(8,128)S(1)} %get-tuple-element.60), channel_id=1, source_target_pairs={{0,1},{4,5},{8,9},{12,13},{1,0},{5,4},{9,8},{13,12},{2,3},{6,7},{1... | collective-permute-start | bytes 393224 | tf_op jit(solution)/shard_map/ppermute | solution.py:274
  57.5 16.3 %collective-permute-start.12 = (f32[128,256]{1,0:T(8,128)S(1)}, f32[128,256]{1,0:T(8,128)S(1)}, u32[]{:S(2)}, u32[]{:S(2)}) collective-permute-start(f32[128,256]{1,0:T(8,128)S(1)} %get-tuple-element.61), channel_id=1, source_target_pairs={{0,5},{4,9},{8,13},{12,0},{1,4},{5,8},{9,12},{13,1},{2,7},{6,11},{... | collective-permute-start | bytes 393224 | tf_op jit(solution)/shard_map/ppermute | solution.py:274
  60.3 16.3 %collective-permute-start.13 = (f32[128,256]{1,0:T(8,128)S(1)}, f32[128,256]{1,0:T(8,128)S(1)}, u32[]{:S(2)}, u32[]{:S(2)}) collective-permute-start(f32[128,256]{1,0:T(8,128)S(1)} %get-tuple-element.62), channel_id=1, source_target_pairs={{0,9},{4,13},{8,0},{12,4},{1,8},{5,12},{9,1},{13,5},{2,11},{6,15},... | collective-permute-start | bytes 393224 | tf_op jit(solution)/shard_map/ppermute | solution.py:274
  68.3 9.3 %collective-permute-start.14 = (f32[128,256]{1,0:T(8,128)S(1)}, f32[128,256]{1,0:T(8,128)S(1)}, u32[]{:S(2)}, u32[]{:S(2)}) collective-permute-start(f32[128,256]{1,0:T(8,128)S(1)} %get-tuple-element.64), channel_id=1, source_target_pairs={{0,13},{4,0},{8,4},{12,8},{1,12},{5,1},{9,5},{13,9},{2,15},{6,2},{... | collective-permute-start | bytes 393224 | tf_op jit(solution)/shard_map/ppermute | solution.py:274

commit v4 on v3

--- a/solution.py
+++ b/solution.py
@@ -7,10 +7,10 @@
 from jax.experimental.pallas import tpu as pltpu
 from jax.sharding import PartitionSpec as P
 
-FIRSTS = (1, 2, 3, 4, 5, 6, 7)
-ORDER = (2, 4, 6, 3, 5, 1, 7)
+FIRSTS = (1, 2, 3, 4, 5, 6, 7, 0)
+ORDER = (2, 4, 6, 3, 5, 0, 1, 7)
 READ = 1
-HELD = 6
+HELD = 7
 EARLY = 5
 TAIL = 8
 EPS = 1e-06
@@ -255,7 +255,16 @@
     sections = n_outer * n_inner // heads
     teams = [[place(s * heads + j) for j in range(heads)] for s in range(sections)]
     position = lax.axis_index("outer") * n_inner + lax.axis_index("inner")
-    section, mine = position // heads, position % heads
+    mine = position % heads
+    if heads % n_inner == 0 and n_outer == sections * (heads // n_inner):
+        owners = [
+            [place((h // n_inner * sections + s) * n_inner + h % n_inner) for h in range(heads)]
+            for s in range(sections)
+        ]
+        outer = lax.axis_index("outer")
+        section, head = outer % sections, outer // sections * n_inner + lax.axis_index("inner")
+    else:
+        owners, section, head = teams, position // heads, mine
     scalars = lambda *xs: jnp.stack([jnp.asarray(x).astype(jnp.int32) for x in xs])
     gates = (retain.T, step.T, momentum.T)
 
@@ -269,15 +278,12 @@
             compiler_params=LIMIT,
         )(*given)
 
-    def shift(piece, s):
-        pairs = [(team[j], team[(j + s) % heads]) for team in teams for j in range(heads)]
+    turns = [*ORDER]
+
+    def shift(piece, s, back=False):
+        ends = (owners, teams) if back else (teams, owners)
+        pairs = [(a[j], b[(j + s) % heads]) for a, b in zip(*ends) for j in range(heads)]
         return lax.ppermute(piece, axes, pairs)
-
-    turns = [s for s in ORDER if s < heads]
-
-    def swap(pieces):
-        moved = {0: pieces[0], **{s: shift(pieces[s], s) for s in turns}}
-        return [moved[s] for s in range(heads)]
 
     def behind(xs, y):
         return list(lax.optimization_barrier((*xs, y))[:-1])
@@ -292,15 +298,14 @@
             [pltpu.VMEM(x.shape, x.dtype) for x in given] + [pltpu.SemaphoreType.DMA((len(given),))],
         )
 
-    order = [*FIRSTS, 0]
+    order = [*FIRSTS]
     made = dict(zip(order, make(order, (keys, values, *gates))))
-    maps = {0: made[0], **{s: shift(made[s], s) for s in order[:-1]}}
-    maps = [maps[s] for s in order]
+    maps = [shift(made[s], s) for s in order]
 
     start = jnp.concatenate(
         [
-            lax.dynamic_index_in_dim(init_memory, mine, 0, keepdims=False),
-            lax.dynamic_index_in_dim(init_moment, mine, 0, keepdims=False),
+            lax.dynamic_index_in_dim(init_memory, head, 0, keepdims=False),
+            lax.dynamic_index_in_dim(init_moment, head, 0, keepdims=False),
         ],
         axis=1,
     )
@@ -313,7 +318,7 @@
             shape(f32, heads, 2 * width + TAIL, width),
             state,
         ],
-        (scalars(mine), start, *maps),
+        (scalars(head), start, *maps),
     )
     entry, other, flag = start, start, section < 0
     for s in range(sections - 1):
@@ -321,15 +326,15 @@
             entry, final = call(
                 functools.partial(final_kernel, heads, width), [state] * 2, (scalars(flag), entry, other, *unpacked)
             )
-        other = lax.ppermute(final, axes, list(zip(teams[s], teams[s + 1])))
+        other = lax.ppermute(final, axes, list(zip(owners[s], owners[s + 1])))
         flag = section == s + 1
     states = call(
         functools.partial(states_kernel, heads, width),
         [state] * heads,
-        (scalars(flag, mine), entry, other, *unpacked),
+        (scalars(flag, head), entry, other, *unpacked),
         scratch=[pltpu.VMEM((heads, width, 2 * width), f32)],
     )
-    pieces, moved = states, {0: states[0]}
+    pieces, moved = states, {}
     for n, s in enumerate(turns):
         if n == READ:
             given = behind((queries, keys, values, *gates), moved[turns[0]])
@@ -345,7 +350,7 @@
                 compiler_params=LIMIT,
             )(*given,)
         piece = pieces[s] if n < HELD else behind([pieces[s]], reads[2])[0]
-        moved[s] = shift(piece, s)
+        moved[s] = shift(piece, s, True)
     states = [moved[s] for s in range(heads)]
     early = call(
         functools.partial(early_kernel, heads),

time: 79.1 us -> 76.2 us (0.963)
  the two profiles are of different devices: /device:TPU:11 before, /device:TPU:1 now
where the time goes in v4:
time: 76.2 us; the launch traced here: 75.9 us
  starting transfers between devices  37.8 us (50%)
  waiting for transfers between devices  23.5 us (31%)
  Pallas kernels  13.5 us (18%)
  local copies, waits for them, and re-layouts  0.91 us (1%)
    ppermute x16, starting transfers between devices, shift(): return lax.ppermute(piece, axes, pairs)  36.5 us
    ppermute x16, waiting for transfers between devices, shift(): return lax.ppermute(piece, axes, pairs)  21.6 us
    pallas_call x5, Pallas kernels, call(): pl.pallas_call(kernel, out_shape=out, in_specs=[SMEM] + [spaces] * (len(g...  9.7 us
    pallas_call x1, Pallas kernels, local(): pl.pallas_call(functools.partial(read_kernel, heads, width), out_shape=[s...  3.77 us
    ppermute x1, waiting for transfers between devices, local(): other = lax.ppermute(final, axes, list(zip(owners[s], owners[s + 1])))  1.85 us
  transfers between devices with their start and end apart: 17, of which 7 were waited for; matrix products, arithmetic and copies ran while one was open for 1% of the time, Pallas kernels for 6%

profile of v4, /device:TPU:1, one launch (start us, length us, event | category | flops | bytes accessed | tf_op | source)
XLA Modules:
  0.0 75.9 jit_solution(16884445300379502523)
XLA Ops:
  0.0 3.9 %shard_map.82 = (f32[392,128]{1,0:T(8,128)S(1)}, f32[392,128]{1,0:T(8,128)S(1)}, f32[392,128]{1,0:T(8,128)S(1)}, f32[392,128]{1,0:T(8,128)S(1)}, f32[392,128]{1,...) custom-call(s32[1]{0:T(128)} %bitcast.mine_ref, bf16[256,1024]{1,0:T(8,128)(2,1)} %k_ref, ...), custom_call_target="tpu_custom_call" | custom-call | tf_op jit(solution)/shard_map/pallas_call | solution.py:272
  3.9 3.7 %collective-permute-start = (f32[392,128]{1,0:T(8,128)S(1)}, f32[392,128]{1,0:T(8,128)S(1)}, u32[]{:S(2)}, u32[]{:S(2)}) collective-permute-start(f32[392,128]{1,0:T(8,128)S(1)} %get-tuple-element.35), channel_id=1, source_target_pairs={{0,4},{4,8},{8,12},{12,2},{1,6},{5,10},{9,14},{13,0},{2,5},{6,9},{... | collective-permute-start | bytes 602120 | tf_op jit(solution)/shard_map/ppermute | solution.py:286
  7.5 2.0 %collective-permute-start.1 = (f32[392,128]{1,0:T(8,128)S(1)}, f32[392,128]{1,0:T(8,128)S(1)}, u32[]{:S(2)}, u32[]{:S(2)}) collective-permute-start(f32[392,128]{1,0:T(8,128)S(1)} %get-tuple-element.36), channel_id=1, source_target_pairs={{0,8},{4,12},{8,2},{12,6},{1,10},{5,14},{9,0},{13,4},{2,9},{6,13},... | collective-permute-start | bytes 602120 | tf_op jit(solution)/shard_map/ppermute | solution.py:286
  9.6 1.1 %collective-permute-start.2 = (f32[392,128]{1,0:T(8,128)S(1)}, f32[392,128]{1,0:T(8,128)S(1)}, u32[]{:S(2)}, u32[]{:S(2)}) collective-permute-start(f32[392,128]{1,0:T(8,128)S(1)} %get-tuple-element.37), channel_id=1, source_target_pairs={{0,12},{4,2},{8,6},{12,10},{1,14},{5,0},{9,4},{13,8},{2,13},{6,3},... | collective-permute-start | bytes 602120 | tf_op jit(solution)/shard_map/ppermute | solution.py:286
  11.3 1.5 %collective-permute-start.4 = (f32[392,128]{1,0:T(8,128)S(1)}, f32[392,128]{1,0:T(8,128)S(1)}, u32[]{:S(2)}, u32[]{:S(2)}) collective-permute-start(f32[392,128]{1,0:T(8,128)S(1)} %get-tuple-element.39), channel_id=1, source_target_pairs={{0,6},{4,10},{8,14},{12,0},{1,4},{5,8},{9,12},{13,2},{2,7},{6,11},... | collective-permute-start | bytes 602120 | tf_op jit(solution)/shard_map/ppermute | solution.py:286
  12.8 0.9 %collective-permute-done.refs_0_ = f32[392,128]{1,0:T(8,128)S(1)} collective-permute-done((f32[392,128]{1,0:T(8,128)S(1)}, f32[392,128]{1,0:T(8,128)S(1)}, u32[]{:S(2)}, u32[]{:S(2)}) %collective-permute-start) | collective-permute-done | bytes 200736 | tf_op jit(solution)/shard_map/ppermute | solution.py:286
  13.7 1.7 %collective-permute-start.5 = (f32[392,128]{1,0:T(8,128)S(1)}, f32[392,128]{1,0:T(8,128)S(1)}, u32[]{:S(2)}, u32[]{:S(2)}) collective-permute-start(f32[392,128]{1,0:T(8,128)S(1)} %get-tuple-element.40), channel_id=1, source_target_pairs={{0,10},{4,14},{8,0},{12,4},{1,8},{5,12},{9,2},{13,6},{2,11},{6,15}... | collective-permute-start | bytes 602120 | tf_op jit(solution)/shard_map/ppermute | solution.py:286
  15.3 8.5 %collective-permute-done.1.refs_1_ = f32[392,128]{1,0:T(8,128)S(1)} collective-permute-done((f32[392,128]{1,0:T(8,128)S(1)}, f32[392,128]{1,0:T(8,128)S(1)}, u32[]{:S(2)}, u32[]{:S(2)}) %collective-permute-start.1) | collective-permute-done | bytes 200736 | tf_op jit(solution)/shard_map/ppermute | solution.py:286
  23.8 5.4 %collective-permute-start.6 = (f32[392,128]{1,0:T(8,128)S(1)}, f32[392,128]{1,0:T(8,128)S(1)}, u32[]{:S(2)}, u32[]{:S(2)}) collective-permute-start(f32[392,128]{1,0:T(8,128)S(1)} %get-tuple-element.41), channel_id=1, source_target_pairs={{0,14},{4,0},{8,4},{12,8},{1,12},{5,2},{9,6},{13,10},{2,15},{6,1},... | collective-permute-start | bytes 602120 | tf_op jit(solution)/shard_map/ppermute | solution.py:286
  29.1 5.2 %collective-permute-start.7 = (f32[392,128]{1,0:T(8,128)S(1)}, f32[392,128]{1,0:T(8,128)S(1)}, u32[]{:S(2)}, u32[]{:S(2)}) collective-permute-start(f32[392,128]{1,0:T(8,128)S(1)} %get-tuple-element.42), channel_id=1, source_target_pairs={{0,0},{4,4},{8,8},{12,12},{1,2},{5,6},{9,10},{13,14},{2,1},{6,5},{... | collective-permute-start | bytes 602120 | tf_op jit(solution)/shard_map/ppermute | solution.py:286
  34.3 0.9 %dynamic-slice_bitcast_fusion = (f32[128,128]{1,0:T(8,128)S(1)}, f32[128,128]{1,0:T(8,128)S(1)}) fusion(f32[8,128,128]{2,1,0:T(8,128)} %param.15, s32[]{:T(128)S(6)} %select_n.23, f32[8,128,128]{2,1,0:T(8,128)} %param.14), kind=kLoop, calls=%fused_computation.1 | loop fusion | bytes 262148 | tf_op jit(solution)/shard_map/jit(dynamic_index_in_dim)/squeeze | solution.py:308
  35.2 4.8 %collective-permute-done.5.refs_5_ = f32[392,128]{1,0:T(8,128)S(1)} collective-permute-done((f32[392,128]{1,0:T(8,128)S(1)}, f32[392,128]{1,0:T(8,128)S(1)}, u32[]{:S(2)}, u32[]{:S(2)}) %collective-permute-start.5) | collective-permute-done | bytes 200736 | tf_op jit(solution)/shard_map/ppermute | solution.py:286
  40.0 1.9 %shard_map.83 = (bf16[8,128,256]{2,1,0:T(8,128)(2,1)S(1)}, bf16[8,128,256]{2,1,0:T(8,128)(2,1)S(1)}, f32[8,264,128]{2,1,0:T(8,128)S(1)}, f32[128,256]{1,0:T(8,128)S(1)}) custom-call(s32[1]{0:T(128)} %bitcast.5.mine_ref, f32[128,256]{1,0:T(8,128)S(1)} %pad_maximum_fusion.entry_ref, f32[392,128]{1,0:T(8,128)S(1)} %collective-permute-done.refs_0_, ...), custom_call_target="tpu_custom_call" | custom-call | tf_op jit(solution)/shard_map/pallas_call | solution.py:272
  41.9 1.3 %collective-permute-start.8 = (f32[128,256]{1,0:T(8,128)S(1)}, f32[128,256]{1,0:T(8,128)S(1)}, u32[]{:S(2)}, u32[]{:S(2)}) collective-permute-start(f32[128,256]{1,0:T(8,128)S(1)} %get-tuple-element.43), channel_id=1, source_target_pairs={{0,1},{4,5},{8,9},{12,13},{2,3},{6,7},{10,11},{14,15},{16,17},{20,... | collective-permute-start | bytes 393224 | tf_op jit(solution)/shard_map/ppermute | solution.py:329
  43.3 1.9 %collective-permute-done.8.other_ref = f32[128,256]{1,0:T(8,128)S(1)} collective-permute-done((f32[128,256]{1,0:T(8,128)S(1)}, f32[128,256]{1,0:T(8,128)S(1)}, u32[]{:S(2)}, u32[]{:S(2)}) %collective-permute-start.8) | collective-permute-done | bytes 131104 | tf_op jit(solution)/shard_map/ppermute | solution.py:329
  45.2 2.0 %shard_map.84 = (f32[128,256]{1,0:T(8,128)S(1)}, f32[128,256]{1,0:T(8,128)S(1)}, f32[128,256]{1,0:T(8,128)S(1)}, f32[128,256]{1,0:T(8,128)S(1)}, f32[128,256]{1,...) custom-call(s32[2]{0:T(128)S(1)} %pad_add_fusion.scalar_ref, ...), custom_call_target="tpu_custom_call" | custom-call | tf_op jit(solution)/shard_map/pallas_call | solution.py:272
  47.1 4.1 %collective-permute-start.9 = (f32[128,256]{1,0:T(8,128)S(1)}, f32[128,256]{1,0:T(8,128)S(1)}, u32[]{:S(2)}, u32[]{:S(2)}) collective-permute-start(f32[128,256]{1,0:T(8,128)S(1)} %get-tuple-element.47), channel_id=1, source_target_pairs={{0,8},{4,12},{8,1},{12,5},{2,9},{6,13},{10,0},{14,4},{1,10},{5,14}... | collective-permute-start | bytes 393224 | tf_op jit(solution)/shard_map/ppermute | solution.py:286
  51.2 2.4 %collective-permute-start.10 = (f32[128,256]{1,0:T(8,128)S(1)}, f32[128,256]{1,0:T(8,128)S(1)}, u32[]{:S(2)}, u32[]{:S(2)}) collective-permute-start(f32[128,256]{1,0:T(8,128)S(1)} %get-tuple-element.57), channel_id=1, source_target_pairs={{0,0},{4,4},{8,8},{12,12},{2,1},{6,5},{10,9},{14,13},{1,2},{5,6},{... | collective-permute-start | bytes 393224 | tf_op jit(solution)/shard_map/ppermute | solution.py:286
  53.6 3.5 %collective-permute-start.11 = (f32[128,256]{1,0:T(8,128)S(1)}, f32[128,256]{1,0:T(8,128)S(1)}, u32[]{:S(2)}, u32[]{:S(2)}) collective-permute-start(f32[128,256]{1,0:T(8,128)S(1)} %get-tuple-element.58), channel_id=1, source_target_pairs={{0,4},{4,8},{8,12},{12,1},{2,5},{6,9},{10,13},{14,0},{1,6},{5,10},... | collective-permute-start | bytes 393224 | tf_op jit(solution)/shard_map/ppermute | solution.py:286
  59.1 3.8 %shard_map.85 = (bf16[8,256,256]{2,1,0:T(8,128)(2,1)S(1)}, bf16[8,256,256]{2,1,0:T(8,128)(2,1)S(1)}, f32[8,256,128]{2,1,0:T(8,128)S(1)}) custom-call(bf16[256,1024]{1,0:T(8,128)(2,1)S(1)} %copy-done.2, bf16[256,1024]{1,0:T(8,128)(2,1)S(1)} %copy-done, bf16[256,1024]{1,0:T(8,128)(2,1)S(1)} %copy-done.1, f32[8,256]{1,0:T(8,128)S(1)} %bitcast.11, ...), custom_call_target="tpu_custom_call" | custom-call | tf_op jit(solution)/shard_map/pallas_call | solution.py:341
  62.9 3.5 %collective-permute-start.15 = (f32[128,256]{1,0:T(8,128)S(1)}, f32[128,256]{1,0:T(8,128)S(1)}, u32[]{:S(2)}, u32[]{:S(2)}) collective-permute-start(f32[128,256]{1,0:T(8,128)S(1)} %get-tuple-element.62), channel_id=1, source_target_pairs={{0,9},{4,13},{8,0},{12,4},{2,8},{6,12},{10,1},{14,5},{1,11},{5,15}... | collective-permute-start | bytes 393224 | tf_op jit(solution)/shard_map/ppermute | solution.py:286
  67.3 5.7 %collective-permute-done.15.refs_1_ = f32[128,256]{1,0:T(8,128)S(1)} collective-permute-done((f32[128,256]{1,0:T(8,128)S(1)}, f32[128,256]{1,0:T(8,128)S(1)}, u32[]{:S(2)}, u32[]{:S(2)}) %collective-permute-start.15) | collective-permute-done | bytes 131104 | tf_op jit(solution)/shard_map/ppermute | solution.py:286
  73.0 1.6 %collective-permute-done.16.refs_2_ = f32[128,256]{1,0:T(8,128)S(1)} collective-permute-done((f32[128,256]{1,0:T(8,128)S(1)}, f32[128,256]{1,0:T(8,128)S(1)}, u32[]{:S(2)}, u32[]{:S(2)}) %collective-permute-start.16) | collective-permute-done | bytes 131104 | tf_op jit(solution)/shard_map/ppermute | solution.py:286
  74.6 1.3 %shard_map.87 = bf16[256,1024]{1,0:T(8,128)(2,1)} custom-call(s32[1]{0:T(128)} %bitcast.mine_ref, bf16[8,256,256]{2,1,0:T(8,128)(2,1)S(1)} %get-tuple-element.54.read_high_ref, bf16[8,256,256]{2,1,0:T(8,128)(2,1)S(1)} %get-tuple-element.55.read_low_ref, f32[8,256,128]{2,1,0:T(8,128)S(1)} %get-tuple-element.56.base_ref, ...), custom_call_target="tpu_custom_call" | custom-call | tf_op jit(solution)/shard_map/pallas_call | solution.py:272
  (31 shorter events, 3.7 us)
Async XLA Ops:
  3.9 9.8 %collective-permute-start = (f32[392,128]{1,0:T(8,128)S(1)}, f32[392,128]{1,0:T(8,128)S(1)}, u32[]{:S(2)}, u32[]{:S(2)}) collective-permute-start(f32[392,128]{1,0:T(8,128)S(1)} %get-tuple-element.35), channel_id=1, source_target_pairs={{0,4},{4,8},{8,12},{12,2},{1,6},{5,10},{9,14},{13,0},{2,5},{6,9},{... | collective-permute-start | bytes 602120 | tf_op jit(solution)/shard_map/ppermute | solution.py:286
  7.5 16.2 %collective-permute-start.1 = (f32[392,128]{1,0:T(8,128)S(1)}, f32[392,128]{1,0:T(8,128)S(1)}, u32[]{:S(2)}, u32[]{:S(2)}) collective-permute-start(f32[392,128]{1,0:T(8,128)S(1)} %get-tuple-element.36), channel_id=1, source_target_pairs={{0,8},{4,12},{8,2},{12,6},{1,10},{5,14},{9,0},{13,4},{2,9},{6,13},... | collective-permute-start | bytes 602120 | tf_op jit(solution)/shard_map/ppermute | solution.py:286
  9.6 19.6 %collective-permute-start.2 = (f32[392,128]{1,0:T(8,128)S(1)}, f32[392,128]{1,0:T(8,128)S(1)}, u32[]{:S(2)}, u32[]{:S(2)}) collective-permute-start(f32[392,128]{1,0:T(8,128)S(1)} %get-tuple-element.37), channel_id=1, source_target_pairs={{0,12},{4,2},{8,6},{12,10},{1,14},{5,0},{9,4},{13,8},{2,13},{6,3},... | collective-permute-start | bytes 602120 | tf_op jit(solution)/shard_map/ppermute | solution.py:286
  10.6 24.6 %collective-permute-start.3 = (f32[392,128]{1,0:T(8,128)S(1)}, f32[392,128]{1,0:T(8,128)S(1)}, u32[]{:S(2)}, u32[]{:S(2)}) collective-permute-start(f32[392,128]{1,0:T(8,128)S(1)} %get-tuple-element.38), channel_id=1, source_target_pairs={{0,2},{4,6},{8,10},{12,14},{1,0},{5,4},{9,8},{13,12},{2,3},{6,7},{... | collective-permute-start | bytes 602120 | tf_op jit(solution)/shard_map/ppermute | solution.py:286
  11.3 23.9 %collective-permute-start.4 = (f32[392,128]{1,0:T(8,128)S(1)}, f32[392,128]{1,0:T(8,128)S(1)}, u32[]{:S(2)}, u32[]{:S(2)}) collective-permute-start(f32[392,128]{1,0:T(8,128)S(1)} %get-tuple-element.39), channel_id=1, source_target_pairs={{0,6},{4,10},{8,14},{12,0},{1,4},{5,8},{9,12},{13,2},{2,7},{6,11},... | collective-permute-start | bytes 602120 | tf_op jit(solution)/shard_map/ppermute | solution.py:286
  13.7 26.3 %collective-permute-start.5 = (f32[392,128]{1,0:T(8,128)S(1)}, f32[392,128]{1,0:T(8,128)S(1)}, u32[]{:S(2)}, u32[]{:S(2)}) collective-permute-start(f32[392,128]{1,0:T(8,128)S(1)} %get-tuple-element.40), channel_id=1, source_target_pairs={{0,10},{4,14},{8,0},{12,4},{1,8},{5,12},{9,2},{13,6},{2,11},{6,15}... | collective-permute-start | bytes 602120 | tf_op jit(solution)/shard_map/ppermute | solution.py:286
  23.8 16.2 %collective-permute-start.6 = (f32[392,128]{1,0:T(8,128)S(1)}, f32[392,128]{1,0:T(8,128)S(1)}, u32[]{:S(2)}, u32[]{:S(2)}) collective-permute-start(f32[392,128]{1,0:T(8,128)S(1)} %get-tuple-element.41), channel_id=1, source_target_pairs={{0,14},{4,0},{8,4},{12,8},{1,12},{5,2},{9,6},{13,10},{2,15},{6,1},... | collective-permute-start | bytes 602120 | tf_op jit(solution)/shard_map/ppermute | solution.py:286
  29.1 10.9 %collective-permute-start.7 = (f32[392,128]{1,0:T(8,128)S(1)}, f32[392,128]{1,0:T(8,128)S(1)}, u32[]{:S(2)}, u32[]{:S(2)}) collective-permute-start(f32[392,128]{1,0:T(8,128)S(1)} %get-tuple-element.42), channel_id=1, source_target_pairs={{0,0},{4,4},{8,8},{12,12},{1,2},{5,6},{9,10},{13,14},{2,1},{6,5},{... | collective-permute-start | bytes 602120 | tf_op jit(solution)/shard_map/ppermute | solution.py:286
  41.9 3.2 %collective-permute-start.8 = (f32[128,256]{1,0:T(8,128)S(1)}, f32[128,256]{1,0:T(8,128)S(1)}, u32[]{:S(2)}, u32[]{:S(2)}) collective-permute-start(f32[128,256]{1,0:T(8,128)S(1)} %get-tuple-element.43), channel_id=1, source_target_pairs={{0,1},{4,5},{8,9},{12,13},{2,3},{6,7},{10,11},{14,15},{16,17},{20,... | collective-permute-start | bytes 393224 | tf_op jit(solution)/shard_map/ppermute | solution.py:329
  45.1 13.9 %copy-start = (bf16[256,1024]{1,0:T(8,128)(2,1)S(1)}, bf16[256,1024]{1,0:T(8,128)(2,1)}, u32[]{:S(2)}) copy-start(bf16[256,1024]{1,0:T(8,128)(2,1)} %k_ref) | copy-start | bytes 1572868
  45.1 13.9 %copy-start.1 = (bf16[256,1024]{1,0:T(8,128)(2,1)S(1)}, bf16[256,1024]{1,0:T(8,128)(2,1)}, u32[]{:S(2)}) copy-start(bf16[256,1024]{1,0:T(8,128)(2,1)} %v_ref) | copy-start | bytes 1572868
  45.1 13.9 %copy-start.2 = (bf16[256,1024]{1,0:T(8,128)(2,1)S(1)}, bf16[256,1024]{1,0:T(8,128)(2,1)}, u32[]{:S(2)}) copy-start(bf16[256,1024]{1,0:T(8,128)(2,1)} %q_ref) | copy-start | bytes 1572868
  45.1 13.9 %copy-start.3 = (f32[256,8]{0,1:T(8,128)S(1)}, f32[256,8]{0,1:T(8,128)}, u32[]{:S(2)}) copy-start(f32[256,8]{0,1:T(8,128)} %param.11) | copy-start | bytes 24580
  45.1 13.9 %copy-start.4 = (f32[256,8]{0,1:T(8,128)S(1)}, f32[256,8]{0,1:T(8,128)}, u32[]{:S(2)}) copy-start(f32[256,8]{0,1:T(8,128)} %param.12) | copy-start | bytes 24580
  45.1 13.9 %copy-start.5 = (f32[256,8]{0,1:T(8,128)S(1)}, f32[256,8]{0,1:T(8,128)}, u32[]{:S(2)}) copy-start(f32[256,8]{0,1:T(8,128)} %param.13) | copy-start | bytes 24580
  47.1 11.1 %collective-permute-start.9 = (f32[128,256]{1,0:T(8,128)S(1)}, f32[128,256]{1,0:T(8,128)S(1)}, u32[]{:S(2)}, u32[]{:S(2)}) collective-permute-start(f32[128,256]{1,0:T(8,128)S(1)} %get-tuple-element.47), channel_id=1, source_target_pairs={{0,8},{4,12},{8,1},{12,5},{2,9},{6,13},{10,0},{14,4},{1,10},{5,14}... | collective-permute-start | bytes 393224 | tf_op jit(solution)/shard_map/ppermute | solution.py:286
  51.2 11.7 %collective-permute-start.10 = (f32[128,256]{1,0:T(8,128)S(1)}, f32[128,256]{1,0:T(8,128)S(1)}, u32[]{:S(2)}, u32[]{:S(2)}) collective-permute-start(f32[128,256]{1,0:T(8,128)S(1)} %get-tuple-element.57), channel_id=1, source_target_pairs={{0,0},{4,4},{8,8},{12,12},{2,1},{6,5},{10,9},{14,13},{1,2},{5,6},{... | collective-permute-start | bytes 393224 | tf_op jit(solution)/shard_map/ppermute | solution.py:286
  53.6 12.8 %collective-permute-start.11 = (f32[128,256]{1,0:T(8,128)S(1)}, f32[128,256]{1,0:T(8,128)S(1)}, u32[]{:S(2)}, u32[]{:S(2)}) collective-permute-start(f32[128,256]{1,0:T(8,128)S(1)} %get-tuple-element.58), channel_id=1, source_target_pairs={{0,4},{4,8},{8,12},{12,1},{2,5},{6,9},{10,13},{14,0},{1,6},{5,10},... | collective-permute-start | bytes 393224 | tf_op jit(solution)/shard_map/ppermute | solution.py:286
  57.1 9.3 %collective-permute-start.12 = (f32[128,256]{1,0:T(8,128)S(1)}, f32[128,256]{1,0:T(8,128)S(1)}, u32[]{:S(2)}, u32[]{:S(2)}) collective-permute-start(f32[128,256]{1,0:T(8,128)S(1)} %get-tuple-element.59), channel_id=1, source_target_pairs={{0,12},{4,1},{8,5},{12,9},{2,13},{6,0},{10,4},{14,8},{1,14},{5,3},... | collective-permute-start | bytes 393224 | tf_op jit(solution)/shard_map/ppermute | solution.py:286
  57.7 8.7 %collective-permute-start.13 = (f32[128,256]{1,0:T(8,128)S(1)}, f32[128,256]{1,0:T(8,128)S(1)}, u32[]{:S(2)}, u32[]{:S(2)}) collective-permute-start(f32[128,256]{1,0:T(8,128)S(1)} %get-tuple-element.60), channel_id=1, source_target_pairs={{0,1},{4,5},{8,9},{12,13},{2,0},{6,4},{10,8},{14,12},{1,3},{5,7},{... | collective-permute-start | bytes 393224 | tf_op jit(solution)/shard_map/ppermute | solution.py:286
  58.2 9.2 %collective-permute-start.14 = (f32[128,256]{1,0:T(8,128)S(1)}, f32[128,256]{1,0:T(8,128)S(1)}, u32[]{:S(2)}, u32[]{:S(2)}) collective-permute-start(f32[128,256]{1,0:T(8,128)S(1)} %get-tuple-element.61), channel_id=1, source_target_pairs={{0,5},{4,9},{8,13},{12,0},{2,4},{6,8},{10,12},{14,1},{1,7},{5,11},... | collective-permute-start | bytes 393224 | tf_op jit(solution)/shard_map/ppermute | solution.py:286
  62.9 10.1 %collective-permute-start.15 = (f32[128,256]{1,0:T(8,128)S(1)}, f32[128,256]{1,0:T(8,128)S(1)}, u32[]{:S(2)}, u32[]{:S(2)}) collective-permute-start(f32[128,256]{1,0:T(8,128)S(1)} %get-tuple-element.62), channel_id=1, source_target_pairs={{0,9},{4,13},{8,0},{12,4},{2,8},{6,12},{10,1},{14,5},{1,11},{5,15}... | collective-permute-start | bytes 393224 | tf_op jit(solution)/shard_map/ppermute | solution.py:286
  66.4 8.2 %collective-permute-start.16 = (f32[128,256]{1,0:T(8,128)S(1)}, f32[128,256]{1,0:T(8,128)S(1)}, u32[]{:S(2)}, u32[]{:S(2)}) collective-permute-start(f32[128,256]{1,0:T(8,128)S(1)} %get-tuple-element.64), channel_id=1, source_target_pairs={{0,13},{4,0},{8,4},{12,8},{2,12},{6,1},{10,5},{14,9},{1,15},{5,2},... | collective-permute-start | bytes 393224 | tf_op jit(solution)/shard_map/ppermute | solution.py:286

commit v5 on v4

--- a/solution.py
+++ b/solution.py
@@ -10,7 +10,7 @@
 FIRSTS = (1, 2, 3, 4, 5, 6, 7, 0)
 ORDER = (2, 4, 6, 3, 5, 0, 1, 7)
 READ = 1
-HELD = 7
+HELD = 8
 EARLY = 5
 TAIL = 8
 EPS = 1e-06

time: 76.2 us -> 75.6 us (level); the launches traced: 75.9 us -> 74.4 us
  waiting for transfers between devices: 23.5 us -> 21.9 us
    ppermute x16, waiting for transfers between devices: 21.6 us -> 20.1 us  [shift(): return lax.ppermute(piece, axes, pairs)]
  transfers between devices with their start and end apart: 17 -> 17, of which waited for: 7 -> 6; matrix products, arithmetic and copies ran while one was open for 1% -> 1% of each run, Pallas kernels for 6% -> 6%
where the time goes in v5:
time: 75.6 us; the launch traced here: 74.4 us
  starting transfers between devices  37.8 us (50%)
  waiting for transfers between devices  21.9 us (29%)
  Pallas kernels  13.5 us (18%)
  local copies, waits for them, and re-layouts  0.91 us (1%)
    ppermute x16, starting transfers between devices, shift(): return lax.ppermute(piece, axes, pairs)  36.5 us
    ppermute x16, waiting for transfers between devices, shift(): return lax.ppermute(piece, axes, pairs)  20.1 us
    pallas_call x5, Pallas kernels, call(): pl.pallas_call(kernel, out_shape=out, in_specs=[SMEM] + [spaces] * (len(g...  9.71 us
    pallas_call x1, Pallas kernels, local(): pl.pallas_call(functools.partial(read_kernel, heads, width), out_shape=[s...  3.77 us
    ppermute x1, waiting for transfers between devices, local(): other = lax.ppermute(final, axes, list(zip(owners[s], owners[s + 1])))  1.85 us
  transfers between devices with their start and end apart: 17, of which 6 were waited for; matrix products, arithmetic and copies ran while one was open for 1% of the time, Pallas kernels for 6%

profile of v5, /device:TPU:1, one launch (start us, length us, event | category | flops | bytes accessed | tf_op | source)
XLA Modules:
  0.0 74.4 jit_solution(18123829119789908274)
XLA Ops:
  0.0 3.9 %shard_map.82 = (f32[392,128]{1,0:T(8,128)S(1)}, f32[392,128]{1,0:T(8,128)S(1)}, f32[392,128]{1,0:T(8,128)S(1)}, f32[392,128]{1,0:T(8,128)S(1)}, f32[392,128]{1,...) custom-call(s32[1]{0:T(128)} %bitcast.mine_ref, bf16[256,1024]{1,0:T(8,128)(2,1)} %k_ref, ...), custom_call_target="tpu_custom_call" | custom-call | tf_op jit(solution)/shard_map/pallas_call | solution.py:272
  3.9 3.7 %collective-permute-start = (f32[392,128]{1,0:T(8,128)S(1)}, f32[392,128]{1,0:T(8,128)S(1)}, u32[]{:S(2)}, u32[]{:S(2)}) collective-permute-start(f32[392,128]{1,0:T(8,128)S(1)} %get-tuple-element.34), channel_id=1, source_target_pairs={{0,4},{4,8},{8,12},{12,2},{1,6},{5,10},{9,14},{13,0},{2,5},{6,9},{... | collective-permute-start | bytes 602120 | tf_op jit(solution)/shard_map/ppermute | solution.py:286
  7.5 2.0 %collective-permute-start.1 = (f32[392,128]{1,0:T(8,128)S(1)}, f32[392,128]{1,0:T(8,128)S(1)}, u32[]{:S(2)}, u32[]{:S(2)}) collective-permute-start(f32[392,128]{1,0:T(8,128)S(1)} %get-tuple-element.35), channel_id=1, source_target_pairs={{0,8},{4,12},{8,2},{12,6},{1,10},{5,14},{9,0},{13,4},{2,9},{6,13},... | collective-permute-start | bytes 602120 | tf_op jit(solution)/shard_map/ppermute | solution.py:286
  9.6 1.1 %collective-permute-start.2 = (f32[392,128]{1,0:T(8,128)S(1)}, f32[392,128]{1,0:T(8,128)S(1)}, u32[]{:S(2)}, u32[]{:S(2)}) collective-permute-start(f32[392,128]{1,0:T(8,128)S(1)} %get-tuple-element.36), channel_id=1, source_target_pairs={{0,12},{4,2},{8,6},{12,10},{1,14},{5,0},{9,4},{13,8},{2,13},{6,3},... | collective-permute-start | bytes 602120 | tf_op jit(solution)/shard_map/ppermute | solution.py:286
  11.3 1.5 %collective-permute-start.4 = (f32[392,128]{1,0:T(8,128)S(1)}, f32[392,128]{1,0:T(8,128)S(1)}, u32[]{:S(2)}, u32[]{:S(2)}) collective-permute-start(f32[392,128]{1,0:T(8,128)S(1)} %get-tuple-element.38), channel_id=1, source_target_pairs={{0,6},{4,10},{8,14},{12,0},{1,4},{5,8},{9,12},{13,2},{2,7},{6,11},... | collective-permute-start | bytes 602120 | tf_op jit(solution)/shard_map/ppermute | solution.py:286
  12.8 0.9 %collective-permute-done.refs_0_ = f32[392,128]{1,0:T(8,128)S(1)} collective-permute-done((f32[392,128]{1,0:T(8,128)S(1)}, f32[392,128]{1,0:T(8,128)S(1)}, u32[]{:S(2)}, u32[]{:S(2)}) %collective-permute-start) | collective-permute-done | bytes 200736 | tf_op jit(solution)/shard_map/ppermute | solution.py:286
  13.7 1.7 %collective-permute-start.5 = (f32[392,128]{1,0:T(8,128)S(1)}, f32[392,128]{1,0:T(8,128)S(1)}, u32[]{:S(2)}, u32[]{:S(2)}) collective-permute-start(f32[392,128]{1,0:T(8,128)S(1)} %get-tuple-element.39), channel_id=1, source_target_pairs={{0,10},{4,14},{8,0},{12,4},{1,8},{5,12},{9,2},{13,6},{2,11},{6,15}... | collective-permute-start | bytes 602120 | tf_op jit(solution)/shard_map/ppermute | solution.py:286
  15.3 8.5 %collective-permute-done.1.refs_1_ = f32[392,128]{1,0:T(8,128)S(1)} collective-permute-done((f32[392,128]{1,0:T(8,128)S(1)}, f32[392,128]{1,0:T(8,128)S(1)}, u32[]{:S(2)}, u32[]{:S(2)}) %collective-permute-start.1) | collective-permute-done | bytes 200736 | tf_op jit(solution)/shard_map/ppermute | solution.py:286
  23.8 5.4 %collective-permute-start.6 = (f32[392,128]{1,0:T(8,128)S(1)}, f32[392,128]{1,0:T(8,128)S(1)}, u32[]{:S(2)}, u32[]{:S(2)}) collective-permute-start(f32[392,128]{1,0:T(8,128)S(1)} %get-tuple-element.40), channel_id=1, source_target_pairs={{0,14},{4,0},{8,4},{12,8},{1,12},{5,2},{9,6},{13,10},{2,15},{6,1},... | collective-permute-start | bytes 602120 | tf_op jit(solution)/shard_map/ppermute | solution.py:286
  29.1 5.2 %collective-permute-start.7 = (f32[392,128]{1,0:T(8,128)S(1)}, f32[392,128]{1,0:T(8,128)S(1)}, u32[]{:S(2)}, u32[]{:S(2)}) collective-permute-start(f32[392,128]{1,0:T(8,128)S(1)} %get-tuple-element.41), channel_id=1, source_target_pairs={{0,0},{4,4},{8,8},{12,12},{1,2},{5,6},{9,10},{13,14},{2,1},{6,5},{... | collective-permute-start | bytes 602120 | tf_op jit(solution)/shard_map/ppermute | solution.py:286
  34.3 0.9 %dynamic-slice_bitcast_fusion = (f32[128,128]{1,0:T(8,128)S(1)}, f32[128,128]{1,0:T(8,128)S(1)}) fusion(f32[8,128,128]{2,1,0:T(8,128)} %param.15, s32[]{:T(128)S(6)} %select_n.23, f32[8,128,128]{2,1,0:T(8,128)} %param.14), kind=kLoop, calls=%fused_computation.1 | loop fusion | bytes 262148 | tf_op jit(solution)/shard_map/jit(dynamic_index_in_dim)/squeeze | solution.py:308
  35.2 4.8 %collective-permute-done.5.refs_5_ = f32[392,128]{1,0:T(8,128)S(1)} collective-permute-done((f32[392,128]{1,0:T(8,128)S(1)}, f32[392,128]{1,0:T(8,128)S(1)}, u32[]{:S(2)}, u32[]{:S(2)}) %collective-permute-start.5) | collective-permute-done | bytes 200736 | tf_op jit(solution)/shard_map/ppermute | solution.py:286
  40.0 1.9 %shard_map.83 = (bf16[8,128,256]{2,1,0:T(8,128)(2,1)S(1)}, bf16[8,128,256]{2,1,0:T(8,128)(2,1)S(1)}, f32[8,264,128]{2,1,0:T(8,128)S(1)}, f32[128,256]{1,0:T(8,128)S(1)}) custom-call(s32[1]{0:T(128)} %bitcast.5.mine_ref, f32[128,256]{1,0:T(8,128)S(1)} %pad_maximum_fusion.entry_ref, f32[392,128]{1,0:T(8,128)S(1)} %collective-permute-done.refs_0_, ...), custom_call_target="tpu_custom_call" | custom-call | tf_op jit(solution)/shard_map/pallas_call | solution.py:272
  41.9 1.3 %collective-permute-start.8 = (f32[128,256]{1,0:T(8,128)S(1)}, f32[128,256]{1,0:T(8,128)S(1)}, u32[]{:S(2)}, u32[]{:S(2)}) collective-permute-start(f32[128,256]{1,0:T(8,128)S(1)} %get-tuple-element.42), channel_id=1, source_target_pairs={{0,1},{4,5},{8,9},{12,13},{2,3},{6,7},{10,11},{14,15},{16,17},{20,... | collective-permute-start | bytes 393224 | tf_op jit(solution)/shard_map/ppermute | solution.py:329
  43.3 1.9 %collective-permute-done.8.other_ref = f32[128,256]{1,0:T(8,128)S(1)} collective-permute-done((f32[128,256]{1,0:T(8,128)S(1)}, f32[128,256]{1,0:T(8,128)S(1)}, u32[]{:S(2)}, u32[]{:S(2)}) %collective-permute-start.8) | collective-permute-done | bytes 131104 | tf_op jit(solution)/shard_map/ppermute | solution.py:329
  45.2 2.0 %shard_map.84 = (f32[128,256]{1,0:T(8,128)S(1)}, f32[128,256]{1,0:T(8,128)S(1)}, f32[128,256]{1,0:T(8,128)S(1)}, f32[128,256]{1,0:T(8,128)S(1)}, f32[128,256]{1,...) custom-call(s32[2]{0:T(128)S(1)} %pad_add_fusion.scalar_ref, ...), custom_call_target="tpu_custom_call" | custom-call | tf_op jit(solution)/shard_map/pallas_call | solution.py:272
  47.1 4.1 %collective-permute-start.9 = (f32[128,256]{1,0:T(8,128)S(1)}, f32[128,256]{1,0:T(8,128)S(1)}, u32[]{:S(2)}, u32[]{:S(2)}) collective-permute-start(f32[128,256]{1,0:T(8,128)S(1)} %get-tuple-element.46), channel_id=1, source_target_pairs={{0,8},{4,12},{8,1},{12,5},{2,9},{6,13},{10,0},{14,4},{1,10},{5,14}... | collective-permute-start | bytes 393224 | tf_op jit(solution)/shard_map/ppermute | solution.py:286
  51.2 2.4 %collective-permute-start.10 = (f32[128,256]{1,0:T(8,128)S(1)}, f32[128,256]{1,0:T(8,128)S(1)}, u32[]{:S(2)}, u32[]{:S(2)}) collective-permute-start(f32[128,256]{1,0:T(8,128)S(1)} %get-tuple-element.56), channel_id=1, source_target_pairs={{0,0},{4,4},{8,8},{12,12},{2,1},{6,5},{10,9},{14,13},{1,2},{5,6},{... | collective-permute-start | bytes 393224 | tf_op jit(solution)/shard_map/ppermute | solution.py:286
  53.6 3.5 %collective-permute-start.11 = (f32[128,256]{1,0:T(8,128)S(1)}, f32[128,256]{1,0:T(8,128)S(1)}, u32[]{:S(2)}, u32[]{:S(2)}) collective-permute-start(f32[128,256]{1,0:T(8,128)S(1)} %get-tuple-element.57), channel_id=1, source_target_pairs={{0,4},{4,8},{8,12},{12,1},{2,5},{6,9},{10,13},{14,0},{1,6},{5,10},... | collective-permute-start | bytes 393224 | tf_op jit(solution)/shard_map/ppermute | solution.py:286
  58.2 0.9 %collective-permute-start.14 = (f32[128,256]{1,0:T(8,128)S(1)}, f32[128,256]{1,0:T(8,128)S(1)}, u32[]{:S(2)}, u32[]{:S(2)}) collective-permute-start(f32[128,256]{1,0:T(8,128)S(1)} %get-tuple-element.60), channel_id=1, source_target_pairs={{0,5},{4,9},{8,13},{12,0},{2,4},{6,8},{10,12},{14,1},{1,7},{5,11},... | collective-permute-start | bytes 393224 | tf_op jit(solution)/shard_map/ppermute | solution.py:286
  59.1 3.5 %collective-permute-start.15 = (f32[128,256]{1,0:T(8,128)S(1)}, f32[128,256]{1,0:T(8,128)S(1)}, u32[]{:S(2)}, u32[]{:S(2)}) collective-permute-start(f32[128,256]{1,0:T(8,128)S(1)} %get-tuple-element.61), channel_id=1, source_target_pairs={{0,9},{4,13},{8,0},{12,4},{2,8},{6,12},{10,1},{14,5},{1,11},{5,15}... | collective-permute-start | bytes 393224 | tf_op jit(solution)/shard_map/ppermute | solution.py:286
  62.6 3.8 %shard_map.85 = (bf16[8,256,256]{2,1,0:T(8,128)(2,1)S(1)}, bf16[8,256,256]{2,1,0:T(8,128)(2,1)S(1)}, f32[8,256,128]{2,1,0:T(8,128)S(1)}) custom-call(bf16[256,1024]{1,0:T(8,128)(2,1)S(1)} %copy-done.2, bf16[256,1024]{1,0:T(8,128)(2,1)S(1)} %copy-done, bf16[256,1024]{1,0:T(8,128)(2,1)S(1)} %copy-done.1, f32[8,256]{1,0:T(8,128)S(1)} %bitcast.11, ...), custom_call_target="tpu_custom_call" | custom-call | tf_op jit(solution)/shard_map/pallas_call | solution.py:341
  67.5 5.5 %collective-permute-done.15.refs_1_ = f32[128,256]{1,0:T(8,128)S(1)} collective-permute-done((f32[128,256]{1,0:T(8,128)S(1)}, f32[128,256]{1,0:T(8,128)S(1)}, u32[]{:S(2)}, u32[]{:S(2)}) %collective-permute-start.15) | collective-permute-done | bytes 131104 | tf_op jit(solution)/shard_map/ppermute | solution.py:286
  73.0 1.3 %shard_map.87 = bf16[256,1024]{1,0:T(8,128)(2,1)} custom-call(s32[1]{0:T(128)} %bitcast.mine_ref, bf16[8,256,256]{2,1,0:T(8,128)(2,1)S(1)} %get-tuple-element.53.read_high_ref, bf16[8,256,256]{2,1,0:T(8,128)(2,1)S(1)} %get-tuple-element.54.read_low_ref, f32[8,256,128]{2,1,0:T(8,128)S(1)} %get-tuple-element.55.base_ref, ...), custom_call_target="tpu_custom_call" | custom-call | tf_op jit(solution)/shard_map/pallas_call | solution.py:272
  (31 shorter events, 3.0 us)
Async XLA Ops:
  3.9 9.8 %collective-permute-start = (f32[392,128]{1,0:T(8,128)S(1)}, f32[392,128]{1,0:T(8,128)S(1)}, u32[]{:S(2)}, u32[]{:S(2)}) collective-permute-start(f32[392,128]{1,0:T(8,128)S(1)} %get-tuple-element.34), channel_id=1, source_target_pairs={{0,4},{4,8},{8,12},{12,2},{1,6},{5,10},{9,14},{13,0},{2,5},{6,9},{... | collective-permute-start | bytes 602120 | tf_op jit(solution)/shard_map/ppermute | solution.py:286
  7.5 16.2 %collective-permute-start.1 = (f32[392,128]{1,0:T(8,128)S(1)}, f32[392,128]{1,0:T(8,128)S(1)}, u32[]{:S(2)}, u32[]{:S(2)}) collective-permute-start(f32[392,128]{1,0:T(8,128)S(1)} %get-tuple-element.35), channel_id=1, source_target_pairs={{0,8},{4,12},{8,2},{12,6},{1,10},{5,14},{9,0},{13,4},{2,9},{6,13},... | collective-permute-start | bytes 602120 | tf_op jit(solution)/shard_map/ppermute | solution.py:286
  9.6 19.6 %collective-permute-start.2 = (f32[392,128]{1,0:T(8,128)S(1)}, f32[392,128]{1,0:T(8,128)S(1)}, u32[]{:S(2)}, u32[]{:S(2)}) collective-permute-start(f32[392,128]{1,0:T(8,128)S(1)} %get-tuple-element.36), channel_id=1, source_target_pairs={{0,12},{4,2},{8,6},{12,10},{1,14},{5,0},{9,4},{13,8},{2,13},{6,3},... | collective-permute-start | bytes 602120 | tf_op jit(solution)/shard_map/ppermute | solution.py:286
  10.6 24.6 %collective-permute-start.3 = (f32[392,128]{1,0:T(8,128)S(1)}, f32[392,128]{1,0:T(8,128)S(1)}, u32[]{:S(2)}, u32[]{:S(2)}) collective-permute-start(f32[392,128]{1,0:T(8,128)S(1)} %get-tuple-element.37), channel_id=1, source_target_pairs={{0,2},{4,6},{8,10},{12,14},{1,0},{5,4},{9,8},{13,12},{2,3},{6,7},{... | collective-permute-start | bytes 602120 | tf_op jit(solution)/shard_map/ppermute | solution.py:286
  11.3 23.9 %collective-permute-start.4 = (f32[392,128]{1,0:T(8,128)S(1)}, f32[392,128]{1,0:T(8,128)S(1)}, u32[]{:S(2)}, u32[]{:S(2)}) collective-permute-start(f32[392,128]{1,0:T(8,128)S(1)} %get-tuple-element.38), channel_id=1, source_target_pairs={{0,6},{4,10},{8,14},{12,0},{1,4},{5,8},{9,12},{13,2},{2,7},{6,11},... | collective-permute-start | bytes 602120 | tf_op jit(solution)/shard_map/ppermute | solution.py:286
  13.7 26.3 %collective-permute-start.5 = (f32[392,128]{1,0:T(8,128)S(1)}, f32[392,128]{1,0:T(8,128)S(1)}, u32[]{:S(2)}, u32[]{:S(2)}) collective-permute-start(f32[392,128]{1,0:T(8,128)S(1)} %get-tuple-element.39), channel_id=1, source_target_pairs={{0,10},{4,14},{8,0},{12,4},{1,8},{5,12},{9,2},{13,6},{2,11},{6,15}... | collective-permute-start | bytes 602120 | tf_op jit(solution)/shard_map/ppermute | solution.py:286
  23.8 16.2 %collective-permute-start.6 = (f32[392,128]{1,0:T(8,128)S(1)}, f32[392,128]{1,0:T(8,128)S(1)}, u32[]{:S(2)}, u32[]{:S(2)}) collective-permute-start(f32[392,128]{1,0:T(8,128)S(1)} %get-tuple-element.40), channel_id=1, source_target_pairs={{0,14},{4,0},{8,4},{12,8},{1,12},{5,2},{9,6},{13,10},{2,15},{6,1},... | collective-permute-start | bytes 602120 | tf_op jit(solution)/shard_map/ppermute | solution.py:286
  29.1 10.9 %collective-permute-start.7 = (f32[392,128]{1,0:T(8,128)S(1)}, f32[392,128]{1,0:T(8,128)S(1)}, u32[]{:S(2)}, u32[]{:S(2)}) collective-permute-start(f32[392,128]{1,0:T(8,128)S(1)} %get-tuple-element.41), channel_id=1, source_target_pairs={{0,0},{4,4},{8,8},{12,12},{1,2},{5,6},{9,10},{13,14},{2,1},{6,5},{... | collective-permute-start | bytes 602120 | tf_op jit(solution)/shard_map/ppermute | solution.py:286
  41.9 3.2 %collective-permute-start.8 = (f32[128,256]{1,0:T(8,128)S(1)}, f32[128,256]{1,0:T(8,128)S(1)}, u32[]{:S(2)}, u32[]{:S(2)}) collective-permute-start(f32[128,256]{1,0:T(8,128)S(1)} %get-tuple-element.42), channel_id=1, source_target_pairs={{0,1},{4,5},{8,9},{12,13},{2,3},{6,7},{10,11},{14,15},{16,17},{20,... | collective-permute-start | bytes 393224 | tf_op jit(solution)/shard_map/ppermute | solution.py:329
  45.1 17.4 %copy-start = (bf16[256,1024]{1,0:T(8,128)(2,1)S(1)}, bf16[256,1024]{1,0:T(8,128)(2,1)}, u32[]{:S(2)}) copy-start(bf16[256,1024]{1,0:T(8,128)(2,1)} %k_ref) | copy-start | bytes 1572868
  45.1 17.4 %copy-start.1 = (bf16[256,1024]{1,0:T(8,128)(2,1)S(1)}, bf16[256,1024]{1,0:T(8,128)(2,1)}, u32[]{:S(2)}) copy-start(bf16[256,1024]{1,0:T(8,128)(2,1)} %v_ref) | copy-start | bytes 1572868
  45.1 17.4 %copy-start.2 = (bf16[256,1024]{1,0:T(8,128)(2,1)S(1)}, bf16[256,1024]{1,0:T(8,128)(2,1)}, u32[]{:S(2)}) copy-start(bf16[256,1024]{1,0:T(8,128)(2,1)} %q_ref) | copy-start | bytes 1572868
  45.1 17.4 %copy-start.3 = (f32[256,8]{0,1:T(8,128)S(1)}, f32[256,8]{0,1:T(8,128)}, u32[]{:S(2)}) copy-start(f32[256,8]{0,1:T(8,128)} %param.11) | copy-start | bytes 24580
  45.1 17.4 %copy-start.4 = (f32[256,8]{0,1:T(8,128)S(1)}, f32[256,8]{0,1:T(8,128)}, u32[]{:S(2)}) copy-start(f32[256,8]{0,1:T(8,128)} %param.12) | copy-start | bytes 24580
  45.1 17.4 %copy-start.5 = (f32[256,8]{0,1:T(8,128)S(1)}, f32[256,8]{0,1:T(8,128)}, u32[]{:S(2)}) copy-start(f32[256,8]{0,1:T(8,128)} %param.13) | copy-start | bytes 24580
  47.1 11.1 %collective-permute-start.9 = (f32[128,256]{1,0:T(8,128)S(1)}, f32[128,256]{1,0:T(8,128)S(1)}, u32[]{:S(2)}, u32[]{:S(2)}) collective-permute-start(f32[128,256]{1,0:T(8,128)S(1)} %get-tuple-element.46), channel_id=1, source_target_pairs={{0,8},{4,12},{8,1},{12,5},{2,9},{6,13},{10,0},{14,4},{1,10},{5,14}... | collective-permute-start | bytes 393224 | tf_op jit(solution)/shard_map/ppermute | solution.py:286
  51.2 7.8 %collective-permute-start.10 = (f32[128,256]{1,0:T(8,128)S(1)}, f32[128,256]{1,0:T(8,128)S(1)}, u32[]{:S(2)}, u32[]{:S(2)}) collective-permute-start(f32[128,256]{1,0:T(8,128)S(1)} %get-tuple-element.56), channel_id=1, source_target_pairs={{0,0},{4,4},{8,8},{12,12},{2,1},{6,5},{10,9},{14,13},{1,2},{5,6},{... | collective-permute-start | bytes 393224 | tf_op jit(solution)/shard_map/ppermute | solution.py:286
  53.6 8.9 %collective-permute-start.11 = (f32[128,256]{1,0:T(8,128)S(1)}, f32[128,256]{1,0:T(8,128)S(1)}, u32[]{:S(2)}, u32[]{:S(2)}) collective-permute-start(f32[128,256]{1,0:T(8,128)S(1)} %get-tuple-element.57), channel_id=1, source_target_pairs={{0,4},{4,8},{8,12},{12,1},{2,5},{6,9},{10,13},{14,0},{1,6},{5,10},... | collective-permute-start | bytes 393224 | tf_op jit(solution)/shard_map/ppermute | solution.py:286
  57.1 9.3 %collective-permute-start.12 = (f32[128,256]{1,0:T(8,128)S(1)}, f32[128,256]{1,0:T(8,128)S(1)}, u32[]{:S(2)}, u32[]{:S(2)}) collective-permute-start(f32[128,256]{1,0:T(8,128)S(1)} %get-tuple-element.58), channel_id=1, source_target_pairs={{0,12},{4,1},{8,5},{12,9},{2,13},{6,0},{10,4},{14,8},{1,14},{5,3},... | collective-permute-start | bytes 393224 | tf_op jit(solution)/shard_map/ppermute | solution.py:286
  57.7 8.7 %collective-permute-start.13 = (f32[128,256]{1,0:T(8,128)S(1)}, f32[128,256]{1,0:T(8,128)S(1)}, u32[]{:S(2)}, u32[]{:S(2)}) collective-permute-start(f32[128,256]{1,0:T(8,128)S(1)} %get-tuple-element.59), channel_id=1, source_target_pairs={{0,1},{4,5},{8,9},{12,13},{2,0},{6,4},{10,8},{14,12},{1,3},{5,7},{... | collective-permute-start | bytes 393224 | tf_op jit(solution)/shard_map/ppermute | solution.py:286
  58.2 9.3 %collective-permute-start.14 = (f32[128,256]{1,0:T(8,128)S(1)}, f32[128,256]{1,0:T(8,128)S(1)}, u32[]{:S(2)}, u32[]{:S(2)}) collective-permute-start(f32[128,256]{1,0:T(8,128)S(1)} %get-tuple-element.60), channel_id=1, source_target_pairs={{0,5},{4,9},{8,13},{12,0},{2,4},{6,8},{10,12},{14,1},{1,7},{5,11},... | collective-permute-start | bytes 393224 | tf_op jit(solution)/shard_map/ppermute | solution.py:286
  59.1 14.0 %collective-permute-start.15 = (f32[128,256]{1,0:T(8,128)S(1)}, f32[128,256]{1,0:T(8,128)S(1)}, u32[]{:S(2)}, u32[]{:S(2)}) collective-permute-start(f32[128,256]{1,0:T(8,128)S(1)} %get-tuple-element.61), channel_id=1, source_target_pairs={{0,9},{4,13},{8,0},{12,4},{2,8},{6,12},{10,1},{14,5},{1,11},{5,15}... | collective-permute-start | bytes 393224 | tf_op jit(solution)/shard_map/ppermute | solution.py:286
  62.5 10.5 %collective-permute-start.16 = (f32[128,256]{1,0:T(8,128)S(1)}, f32[128,256]{1,0:T(8,128)S(1)}, u32[]{:S(2)}, u32[]{:S(2)}) collective-permute-start(f32[128,256]{1,0:T(8,128)S(1)} %get-tuple-element.62), channel_id=1, source_target_pairs={{0,13},{4,0},{8,4},{12,8},{2,12},{6,1},{10,5},{14,9},{1,15},{5,2},... | collective-permute-start | bytes 393224 | tf_op jit(solution)/shard_map/ppermute | solution.py:286
